TPU v7x, 128 devices: a whole 4x4x4 slice. The times are simulated.
128 devices in a mesh: tok: 8 (over x, core), voc: 16 (over y, z).
Axes of the slice: x: 4, y: 4, z: 4, core: 2. Of those that a mesh axis runs over, the one named last changes fastest.
Arguments:
- tokens_in: bfloat16 [1024, 4096], P(('tok', 'voc')), may hold values from -36 to 36
- gate_raw: float32 [1024, 8], P(('tok', 'voc')), may hold values from 0.05 to 1
- expert_ids: int32 [1024, 8], P(('tok', 'voc')), may hold values from 0 to 63, all different within a row; in each aligned block of 8 rows (0 to 7, 8 to 15, ...) at most 2 rows name the same one
- w_gate: bfloat16 [4096, 49152], P(None, ('tok', 'voc')), may hold values from -0.09375 to 0.09375
- w_up: bfloat16 [4096, 49152], P(None, ('tok', 'voc')), may hold values from -0.09375 to 0.09375
- w_down: bfloat16 [49152, 4096], P(('tok', 'voc')), may hold values from -0.875 to 0.875
- final_gain: float32 [4096], replicated, may hold values from 0.1 to 1.9
- teacher_head: bfloat16 [4096, 77824], P('tok', 'voc')
- student_hidden: bfloat16 [1024, 4096], P('voc', 'tok'), may hold values from -6 to 6
- student_head: bfloat16 [4096, 77824], P('tok', 'voc')
- sampled_ids: int32 [1024], P('tok'), may hold values from 0 to 77823
- token_weight: float32 [1024], P('tok'), may hold values from 2 to 32
Outputs:
- token_loss: float32 [1024], P('tok')
- hidden_grad: bfloat16 [1024, 4096], P('voc', 'tok')
Inputs may be any that keep to these rules, and one draw needn't show every extreme that they name: `expert_ids`: each row names 8 different experts; in the 8 rows of one device no expert is named by more than 2 rows, a bound that some block reaches.
All inputs are finite; a program needn't handle non-finite values.
Results may differ from a plain program's by a relative error of at most 0.01375.
Values may be sent and summed in bfloat16 or wider, within the bound.
A program may use at most 128 MiB of HBM per device.

v0:
```python
import jax
import jax.numpy as jnp
from jax import lax
from jax.sharding import PartitionSpec as P


def route_tables(expert_ids, gate_raw, experts, capacity):
    rows_here, top_k = expert_ids.shape
    flat_ids = expert_ids.reshape(-1)
    one_hot = (flat_ids[:, None] == jnp.arange(experts, dtype=jnp.int32)[None, :]).astype(jnp.int32)
    earlier = jnp.cumsum(one_hot, axis=0, dtype=jnp.int32) - one_hot
    slot_of = jnp.sum(earlier * one_hot, axis=1, dtype=jnp.int32)
    where_to = (flat_ids * capacity + slot_of).reshape(rows_here, top_k)
    columns = jnp.arange(experts * capacity, dtype=jnp.int32)
    matched = where_to[:, :, None] == columns[None, None, :]
    shares = gate_raw / jnp.sum(gate_raw, axis=1, keepdims=True)
    combine_table = jnp.sum(jnp.where(matched, shares[:, :, None], 0.0), axis=1)
    dispatch_table = jnp.transpose(jnp.any(matched, axis=1)).astype(jnp.bfloat16)
    return (dispatch_table, combine_table)


def per_device(
    tokens_in,
    gate_raw,
    expert_ids,
    w_gate,
    w_up,
    w_down,
    final_gain,
    teacher_head,
    student_hidden,
    student_head,
    sampled_ids,
    token_weight,
):
    tok_count = lax.axis_size("tok")
    voc_count = lax.axis_size("voc")
    experts = tok_count * voc_count // 2
    rows_here, top_k = expert_ids.shape
    model_width = tokens_in.shape[1]
    capacity = max(2, 2 * rows_here * top_k // experts)
    dispatch_table, combine_table = route_tables(expert_ids, gate_raw, experts, capacity)
    dispatched = jnp.dot(dispatch_table, tokens_in, preferred_element_type=jnp.float32).astype(
        jnp.bfloat16
    )
    outgoing = jnp.repeat(dispatched.reshape(experts, capacity, model_width), 2, axis=0)
    arrived = lax.all_to_all(outgoing, ("tok", "voc"), split_axis=0, concat_axis=0, tiled=True)
    expert_rows = arrived.reshape(2 * experts * capacity, model_width)
    gate_part = jnp.dot(expert_rows, w_gate, preferred_element_type=jnp.float32)
    up_part = jnp.dot(expert_rows, w_up, preferred_element_type=jnp.float32)
    hidden_units = (jax.nn.silu(gate_part) * up_part).astype(jnp.bfloat16)
    partial_out = (
        jnp.dot(hidden_units, w_down, preferred_element_type=jnp.float32)
        .astype(jnp.bfloat16)
        .reshape(2 * experts, capacity, model_width)
    )
    returned = lax.all_to_all(partial_out, ("tok", "voc"), split_axis=0, concat_axis=0, tiled=True)
    pair_sum = jnp.sum(
        returned.astype(jnp.float32).reshape(experts, 2, capacity, model_width), axis=1
    ).reshape(experts * capacity, model_width)
    expert_mix = jnp.dot(combine_table, pair_sum, precision=lax.Precision.HIGHEST)
    residual_sum = tokens_in.astype(jnp.float32) + expert_mix
    inverse = lax.rsqrt(jnp.mean(residual_sum * residual_sum, axis=1, keepdims=True) + 1e-06)
    normed = (residual_sum * inverse * final_gain[None, :]).astype(jnp.bfloat16)
    tok_rows = lax.all_gather(normed, "voc", axis=0, tiled=True)
    teacher_cols = lax.all_to_all(tok_rows, "tok", split_axis=1, concat_axis=0, tiled=True)
    student_all = lax.all_gather(student_hidden, "voc", axis=0, tiled=True)
    vocab_local = teacher_head.shape[1]
    rows_piece = teacher_cols
    teacher_logits = lax.psum_scatter(
        jnp.dot(rows_piece, teacher_head, preferred_element_type=jnp.float32).astype(jnp.bfloat16),
        "tok",
        scatter_dimension=0,
        tiled=True,
    ).astype(jnp.float32)
    rows_piece = student_all
    student_logits = lax.psum_scatter(
        jnp.dot(rows_piece, student_head, preferred_element_type=jnp.float32),
        "tok",
        scatter_dimension=0,
        tiled=True,
    )
    differ = student_logits - teacher_logits
    vocab_start = lax.axis_index("voc") * vocab_local
    picked = sampled_ids[:, None] - vocab_start == jnp.arange(vocab_local, dtype=jnp.int32)[None, :]
    picked_s = jnp.sum(jnp.where(picked, student_logits, 0.0), axis=1)
    picked_t = jnp.sum(jnp.where(picked, teacher_logits, 0.0), axis=1)
    local_tmax = jnp.max(teacher_logits, axis=1)
    local_smax = jnp.max(student_logits, axis=1)
    teacher_max, student_max = lax.pmax((local_tmax, local_smax), "voc")
    student_exp = jnp.exp(student_logits - student_max[:, None])
    teacher_sum, student_sum, cross_sum, picked_s, picked_t = lax.psum(
        (
            jnp.sum(jnp.exp(teacher_logits - teacher_max[:, None]), axis=1),
            jnp.sum(student_exp, axis=1),
            jnp.sum(student_exp * differ, axis=1),
            picked_s,
            picked_t,
        ),
        "voc",
    )
    teacher_norm = teacher_max + jnp.log(teacher_sum)
    student_norm = student_max + jnp.log(student_sum)
    expect = cross_sum / student_sum
    token_loss = (
        expect - student_norm + teacher_norm + (picked_s - student_norm) - (picked_t - teacher_norm)
    )
    student_prob = jnp.exp(student_logits - student_norm[:, None])
    logit_grad = (
        token_weight[:, None]
        * (student_prob * (differ - expect[:, None]) + picked.astype(jnp.float32) - student_prob)
    ).astype(jnp.bfloat16)
    grad_terms = lax.dot_general(
        lax.all_gather(logit_grad, "tok", axis=0, tiled=True),
        student_head,
        (((1,), (1,)), ((), ())),
        preferred_element_type=jnp.float32,
    )
    hidden_grad = lax.psum_scatter(
        grad_terms.astype(jnp.bfloat16), "voc", scatter_dimension=0, tiled=True
    )
    return (token_loss, hidden_grad)


def solution(mesh):
    in_specs = (
        P(("tok", "voc"), None),
        P(("tok", "voc"), None),
        P(("tok", "voc"), None),
        P(None, ("tok", "voc")),
        P(None, ("tok", "voc")),
        P(("tok", "voc"), None),
        P(),
        P("tok", "voc"),
        P("voc", "tok"),
        P("tok", "voc"),
        P("tok"),
        P("tok"),
    )
    out_specs = (P("tok"), P("voc", "tok"))
    return jax.shard_map(
        per_device, mesh=mesh, in_specs=in_specs, out_specs=out_specs, check_vma=False
    )
```

profile of v0, /device:TPU:17, one launch (start us, length us, event | category | flops | bytes accessed | tf_op | source)
XLA Modules:
  0.0 609.7 jit_solution(13637765129616562563)
XLA Ops:
  7.2 0.9 eq.20
  9.3 2.3 convolution_convert_fusion.2
  11.6 2.5 reshape.54
  14.2 3.7 broadcast_in_dim.21
  17.9 39.2 %all_to_all.29 = bf16[128,2,4096]{2,1,0:T(2,128)(2,1)} all-to-all(bf16[128,2,4096]{2,1,0:T(2,128)(2,1)S(1)} %bitcast.26), channel_id=1, replica_groups=mesh['tok'=8,'voc'=16] {'tok','voc'}, dimensions={0} | all-to-all | bytes 4194304 | tf_op jit(solution)/shard_map/all_to_all | solution.py:47
  57.1 4.1 reshape.56
  61.2 3.8 fusion.15
  65.0 6.3 %convolution_convert_fusion.1 = bf16[256,4096]{1,0:T(8,128)(2,1)} fusion(bf16[384,4096]{1,0:T(8,128)(2,1)S(1)} %copy-done, bf16[256,4096]{1,0:T(8,128)(2,1)} %reshape.56, bf16[4096,384]{1,0:T(8,128)(2,1)} %param.16, f32[256,384]{1,0:T(8,128)S(1)} %fusion.15), kind=kOutput, calls=%fused_computation.1 | convolution fusion | flops 1612251136 | bytes 10878976 | tf_op jit(solution)/shard_map/dot_general | solution.py:53
  71.2 4.4 reshape.57
  75.6 5.9 all-to-all-start.1
  82.1 28.1 %all-to-all-done.1 = bf16[128,2,4096]{2,1,0:T(2,128)(2,1)S(1)} async-done(((bf16[128,2,4096]{2,1,0:T(2,128)(2,1)}), bf16[128,2,4096]{2,1,0:T(2,128)(2,1)S(1)}, u32[]{:S(2)}, u32[]{:S(2)}) %all-to-all-start.1) | async-done | bytes 2097184 | tf_op jit(solution)/shard_map/all_to_all | solution.py:57
  110.2 4.1 convert_reduce_fusion
  114.3 2.7 reshape.60
  117.1 1.2 multiply_reduce_fusion.1
  119.0 37.4 %all-gather.6.cloned.1.call-done = bf16[128,4096]{1,0:T(8,128)(2,1)} async-done(((bf16[8,4096]{1,0:T(8,128)(2,1)}), bf16[128,4096]{1,0:T(8,128)(2,1)}) %all-gather.6.cloned.1.call-update) | async-done | bytes 1048592 | tf_op jit(solution)/shard_map/all_gather | solution.py:65
  156.5 2.3 copy.18
  158.8 7.0 %all-to-all-start.2 = ((bf16[128,8,512]{2,0,1:T(8,128)(2,1)}), bf16[128,8,512]{2,0,1:T(8,128)(2,1)S(1)}, u32[]{:S(2)}, u32[]{:S(2)}) async-start(bf16[128,8,512]{2,0,1:T(8,128)(2,1)} %bitcast.25), calls=%async_computation.3 | async-start | bytes 2097152 | tf_op jit(solution)/shard_map/all_to_all | solution.py:66
  166.6 14.2 %all-to-all-done.2 = bf16[128,8,512]{2,0,1:T(8,128)(2,1)S(1)} async-done(((bf16[128,8,512]{2,0,1:T(8,128)(2,1)}), bf16[128,8,512]{2,0,1:T(8,128)(2,1)S(1)}, u32[]{:S(2)}, u32[]{:S(2)}) %all-to-all-start.2) | async-done | bytes 1048608 | tf_op jit(solution)/shard_map/all_to_all | solution.py:66
  180.8 10.2 %convolution_convert_fusion = bf16[1024,4864]{1,0:T(8,128)(2,1)} fusion(bf16[1024,512]{1,0:T(8,128)(2,1)S(1)} %bitcast.27, bf16[512,4864]{1,0:T(8,128)(2,1)} %param.19), kind=kOutput, calls=%fused_computation | convolution fusion | flops 5105254400 | bytes 15990784 | tf_op jit(solution)/shard_map/dot_general | solution.py:71
  191.0 17.5 %all-gather.4.cloned.1.call-done = bf16[1024,512]{1,0:T(8,128)(2,1)} async-done(((bf16[64,512]{1,0:T(8,128)(2,1)}), bf16[1024,512]{1,0:T(8,128)(2,1)}) %all-gather.4.cloned.1.call-update) | async-done | bytes 1048592 | tf_op jit(solution)/shard_map/all_gather | solution.py:67
  208.5 12.1 %fusion.14 = f32[1024,4864]{1,0:T(8,128)} fusion(bf16[1024,512]{1,0:T(8,128)(2,1)} %all-gather.4.cloned.1.call-done, bf16[512,4864]{1,0:T(8,128)(2,1)} %param.21), kind=kOutput, calls=%fused_computation.42 | convolution fusion | flops 5100273664 | bytes 25952256 | tf_op jit(solution)/shard_map/dot_general | solution.py:78
  221.2 51.0 %reduce-scatter.6.cloned.1.call-done = bf16[128,4864]{1,0:T(8,128)(2,1)} async-done(((bf16[1024,4864]{1,0:T(8,128)(2,1)}), bf16[128,4864]{1,0:T(8,128)(2,1)}) %reduce-scatter.6.cloned.1.call-update) | async-done | bytes 1245200 | tf_op jit(solution)/shard_map/reduce_scatter | solution.py:70
  272.2 1.5 reduce_max.24
  273.8 107.0 %reduce-scatter.4.cloned.1.call-done = f32[128,4864]{1,0:T(8,128)} async-done(((f32[1024,4864]{1,0:T(8,128)}), f32[128,4864]{1,0:T(8,128)}) %reduce-scatter.4.cloned.1.call-update) | async-done | bytes 2490384 | tf_op jit(solution)/shard_map/reduce_scatter | solution.py:77
  380.8 2.0 reduce_max.23
  382.9 27.0 %all-reduce.1 = (f32[128]{0:T(128)S(1)}, f32[128]{0:T(128)S(1)}) all-reduce(f32[128]{0:T(128)S(1)} %reduce_max.23, bf16[128]{0:T(256)(128)(2,1)S(1)} %reduce_max.24), channel_id=1, replica_groups=mesh['tok'=8,'voc'=16] {'voc'}, use_global_device_ids=true, to_apply=%region_2.3 | all-reduce | flops 256 | bytes 1792 | tf_op jit(solution)/shard_map/pmax | solution.py:90
  409.9 3.6 multiply_reduce_fusion
  413.5 24.5 %all-reduce = (f32[128]{0:T(128)S(1)}, f32[128]{0:T(128)S(1)}, f32[128]{0:T(128)S(1)}, f32[128]{0:T(128)S(1)}, f32[128]{0:T(128)S(1)}) all-reduce(f32[128]{0:T(128)S(1)} %get-tuple-element.5, f32[128]{0:T(128)S(1)} %get-tuple-element.4, f32[128]{0:T(128)S(1)} %get-tuple-element.3, ...), channel_id=1, replica_groups=mesh['tok'=8,'voc'=16] {'voc'}, use_global_device_ids=true, to_apply=%region_22.23 | all-reduce | flops 640 | bytes 5120 | tf_op jit(solution)/shard_map/psum | solution.py:92
  438.4 3.5 multiply_convert_fusion
  442.1 78.1 %all-gather.8.cloned.1.call-done = bf16[1024,4864]{1,0:T(8,128)(2,1)} async-done(((bf16[128,4864]{1,0:T(8,128)(2,1)}), bf16[1024,4864]{1,0:T(8,128)(2,1)}) %all-gather.8.cloned.1.call-update) | async-done | bytes 9961488 | tf_op jit(solution)/shard_map/all_gather | solution.py:114
  520.1 11.1 %convolution_convert_fusion.3 = bf16[1024,512]{1,0:T(8,128)(2,1)} fusion(bf16[1024,4864]{1,0:T(8,128)(2,1)} %all-gather.8.cloned.1.call-done, bf16[512,4864]{1,0:T(8,128)(2,1)} %param.21), kind=kOutput, calls=%fused_computation.17 | convolution fusion | flops 5100797952 | bytes 15990784 | tf_op jit(solution)/shard_map/dot_general | solution.py:113
  531.3 71.5 %reduce-scatter.8.cloned.1.call-done = bf16[64,512]{1,0:T(8,128)(2,1)} async-done(((bf16[1024,512]{1,0:T(8,128)(2,1)}), bf16[64,512]{1,0:T(8,128)(2,1)}) %reduce-scatter.8.cloned.1.call-update) | async-done | bytes 65552 | tf_op jit(solution)/shard_map/reduce_scatter | solution.py:119
  (41 shorter events, 4.6 us)
Async XLA Ops:
  7.2 57.8 %copy-start = (bf16[384,4096]{1,0:T(8,128)(2,1)S(1)}, bf16[384,4096]{1,0:T(8,128)(2,1)}, u32[]{:S(2)}) copy-start(bf16[384,4096]{1,0:T(8,128)(2,1)} %param.17) | copy-start | bytes 9437188
  75.6 6.2 %copy-start.4 = (f32[8,8]{1,0:T(8,128)S(1)}, f32[8,8]{1,0:T(8,128)}, u32[]{:S(2)}) copy-start(f32[8,8]{1,0:T(8,128)} %param.13) | copy-start | bytes 772
  75.6 34.6 %all-to-all-start.1 = ((bf16[128,2,4096]{2,1,0:T(2,128)(2,1)}), bf16[128,2,4096]{2,1,0:T(2,128)(2,1)S(1)}, u32[]{:S(2)}, u32[]{:S(2)}) async-start(bf16[128,2,4096]{2,1,0:T(2,128)(2,1)} %reshape.57), calls=%async_computation.2 | async-start | bytes 4194304 | tf_op jit(solution)/shard_map/all_to_all | solution.py:57
  81.6 74.9 %all-gather.6.cloned.1.call-start = ((), (), s32[]{:S(2)}) async-start(), calls=%async_computation.8 | async-start | bytes 1114112 | tf_op jit(solution)/shard_map/all_gather | solution.py:65
  114.3 2.7 copy-start.3
  114.3 4.0 copy-start.5
  158.8 22.0 %all-to-all-start.2 = ((bf16[128,8,512]{2,0,1:T(8,128)(2,1)}), bf16[128,8,512]{2,0,1:T(8,128)(2,1)S(1)}, u32[]{:S(2)}, u32[]{:S(2)}) async-start(bf16[128,8,512]{2,0,1:T(8,128)(2,1)} %bitcast.25), calls=%async_computation.3 | async-start | bytes 2097152 | tf_op jit(solution)/shard_map/all_to_all | solution.py:66
  165.8 42.7 %all-gather.4.cloned.1.call-start = ((), (), s32[]{:S(2)}) async-start(), calls=%async_computation.6 | async-start | bytes 1114112 | tf_op jit(solution)/shard_map/all_gather | solution.py:67
  166.5 105.7 %reduce-scatter.6.cloned.1.call-start = ((), (), s32[]{:S(2)}) async-start(), calls=%async_computation.9 | async-start | bytes 11206656 | tf_op jit(solution)/shard_map/reduce_scatter | solution.py:70
  191.0 189.9 %reduce-scatter.4.cloned.1.call-start = ((), (), s32[]{:S(2)}) async-start(), calls=%async_computation.7 | async-start | bytes 22413312 | tf_op jit(solution)/shard_map/reduce_scatter | solution.py:77
  220.6 0.7 copy-start.7
  220.6 299.6 %all-gather.8.cloned.1.call-start = ((), (), s32[]{:S(2)}) async-start(), calls=%async_computation.10 | async-start | bytes 11206656 | tf_op jit(solution)/shard_map/all_gather | solution.py:114
  380.8 29.1 %copy-start.2 = (f32[128,4864]{1,0:T(8,128)S(1)}, f32[128,4864]{1,0:T(8,128)}, u32[]{:S(2)}) copy-start(f32[128,4864]{1,0:T(8,128)} %reduce-scatter.4.cloned.1.call-done) | copy-start | bytes 7471108
  382.9 55.6 %copy-start.6 = (f32[128]{0:T(128)S(1)}, f32[128]{0:T(128)}, u32[]{:S(2)}) copy-start(f32[128]{0:T(128)} %param.23) | copy-start | bytes 1540
  442.0 160.8 %reduce-scatter.8.cloned.1.call-start = ((), (), s32[]{:S(2)}) async-start(), calls=%async_computation.11 | async-start | bytes 1114112 | tf_op jit(solution)/shard_map/reduce_scatter | solution.py:119
  520.1 82.7 %copy-start.1 = (bf16[384,4096]{1,0:T(8,128)(2,1)S(1)}, bf16[384,4096]{1,0:T(8,128)(2,1)}, u32[]{:S(2)}) copy-start(bf16[384,4096]{1,0:T(8,128)(2,1)} %param.17) | copy-start | bytes 9437188
Sparse Core Ops, SparseCore 0:
  119.2 37.2 all-gather.5
  168.7 39.6 all-gather.3
  210.9 61.3 reduce-scatter.5
  274.6 106.2 reduce-scatter.3
  442.1 77.9 all-gather.7
  531.4 71.3 reduce-scatter.7
where the time goes:
time: 613 us; the launch traced here: 610 us
  waiting for transfers between devices  406 us (66%)
  blocking collectives  90.6 us (15%)
  matrix products  46.9 us (8%)
  local copies, waits for them, and re-layouts  21.4 us (3%)
  other arithmetic  17.5 us (3%)
  between operations  14.2 us (2%)
  starting transfers between devices  13.3 us (2%)
    reduce_scatter x1, waiting for transfers between devices, per_device(): lax.psum_scatter(jnp.dot(rows_piece, student_head, preferred_element_type...  107 us
    all_gather x1, waiting for transfers between devices, per_device(): lax.all_gather(logit_grad, 'tok', axis=0, tiled=True)  78.1 us
    reduce_scatter x1, waiting for transfers between devices, per_device(): lax.psum_scatter(grad_terms.astype(jnp.bfloat16), 'voc', scatter_dimensio...  71.5 us
    reduce_scatter x1, waiting for transfers between devices, per_device(): lax.psum_scatter(jnp.dot(rows_piece, teacher_head, preferred_element_type...  51 us
    all_to_all x1, blocking collectives, per_device(): lax.all_to_all(outgoing, ('tok', 'voc'), split_axis=0, concat_axis=0, til...  39.2 us
    all_gather x1, waiting for transfers between devices, per_device(): tok_rows = lax.all_gather(normed, 'voc', axis=0, tiled=True)  37.4 us
    all_to_all x1, waiting for transfers between devices, per_device(): lax.all_to_all(partial_out, ('tok', 'voc'), split_axis=0, concat_axis=0,...  28.1 us
    pmax x1, blocking collectives, per_device(): teacher_max, student_max = lax.pmax((local_tmax, local_smax), 'voc')  27 us
  transfers between devices with their start and end apart: 8, of which 8 were waited for; matrix products, arithmetic and copies ran while one was open for 4% of the time, Pallas kernels for 0%

commit v1 on v0

--- a/solution.py
+++ b/solution.py
@@ -1,7 +1,12 @@
+import functools
 import jax
 import jax.numpy as jnp
 from jax import lax
+from jax.experimental import pallas as pl
+from jax.experimental.pallas import tpu as pltpu
 from jax.sharding import PartitionSpec as P
+
+MESH = pl.DeviceIdType.MESH
 
 
 def route_tables(expert_ids, gate_raw, experts, capacity):
@@ -17,6 +22,63 @@
     combine_table = jnp.sum(jnp.where(matched, shares[:, :, None], 0.0), axis=1)
     dispatch_table = jnp.transpose(jnp.any(matched, axis=1)).astype(jnp.bfloat16)
     return (dispatch_table, combine_table)
+
+
+def gather_kernel(n, x_ref, out_ref, send_sem, recv_sem, own_sem):
+    t, me = lax.axis_index("tok"), lax.axis_index("voc")
+    barrier = pltpu.get_barrier_semaphore()
+
+    @pl.loop(1, n)
+    def _(k):
+        pl.semaphore_signal(
+            barrier, inc=1, device_id=(t, lax.rem(me + k, n)), device_id_type=MESH
+        )
+
+    pl.semaphore_wait(barrier, n - 1)
+
+    def copy(k):
+        return pltpu.make_async_remote_copy(
+            src_ref=x_ref,
+            dst_ref=out_ref.at[me],
+            send_sem=send_sem.at[k],
+            recv_sem=recv_sem.at[k],
+            device_id=(t, lax.rem(me + k, n)),
+            device_id_type=MESH,
+        )
+
+    @pl.loop(1, n)
+    def _(k):
+        copy(k).start()
+
+    own = pltpu.make_async_copy(x_ref, out_ref.at[me], own_sem)
+    own.start()
+    own.wait()
+
+    @pl.loop(1, n)
+    def _(k):
+        pltpu.make_async_remote_copy(
+            src_ref=x_ref,
+            dst_ref=out_ref.at[lax.rem(me - k + n, n)],
+            send_sem=send_sem.at[k],
+            recv_sem=recv_sem.at[k],
+            device_id=(t, lax.rem(me + k, n)),
+            device_id_type=MESH,
+        ).wait()
+
+
+def voc_gather(x, n, collective_id):
+    return pl.pallas_call(
+        functools.partial(gather_kernel, n),
+        out_shape=jax.ShapeDtypeStruct((n,) + x.shape, x.dtype),
+        in_specs=[pl.BlockSpec(memory_space=pltpu.VMEM)],
+        out_specs=pl.BlockSpec(memory_space=pltpu.VMEM),
+        scratch_shapes=[
+            pltpu.SemaphoreType.DMA((n,)),
+            pltpu.SemaphoreType.DMA((n,)),
+            pltpu.SemaphoreType.DMA,
+        ],
+        compiler_params=pltpu.CompilerParams(collective_id=collective_id, has_side_effects=True),
+    )(x)
 
 
 def per_device(
@@ -44,6 +106,10 @@
         jnp.bfloat16
     )
     outgoing = jnp.repeat(dispatched.reshape(experts, capacity, model_width), 2, axis=0)
+    student_all = voc_gather(student_hidden, voc_count, 1).reshape(-1, student_hidden.shape[1])
+    student_part = jnp.dot(student_all, student_head, preferred_element_type=jnp.float32)
+    outgoing, student_part = lax.optimization_barrier((outgoing, student_part))
+    student_logits = lax.psum_scatter(student_part, "tok", scatter_dimension=0, tiled=True)
     arrived = lax.all_to_all(outgoing, ("tok", "voc"), split_axis=0, concat_axis=0, tiled=True)
     expert_rows = arrived.reshape(2 * experts * capacity, model_width)
     gate_part = jnp.dot(expert_rows, w_gate, preferred_element_type=jnp.float32)
@@ -62,43 +128,44 @@
     residual_sum = tokens_in.astype(jnp.float32) + expert_mix
     inverse = lax.rsqrt(jnp.mean(residual_sum * residual_sum, axis=1, keepdims=True) + 1e-06)
     normed = (residual_sum * inverse * final_gain[None, :]).astype(jnp.bfloat16)
-    tok_rows = lax.all_gather(normed, "voc", axis=0, tiled=True)
+    tok_rows = voc_gather(normed, voc_count, 2).reshape(-1, model_width)
     teacher_cols = lax.all_to_all(tok_rows, "tok", split_axis=1, concat_axis=0, tiled=True)
-    student_all = lax.all_gather(student_hidden, "voc", axis=0, tiled=True)
     vocab_local = teacher_head.shape[1]
-    rows_piece = teacher_cols
+    teacher_part = jnp.dot(teacher_cols, teacher_head, preferred_element_type=jnp.float32)
+    teacher_part, student_logits = lax.optimization_barrier(
+        (teacher_part.astype(jnp.bfloat16), student_logits)
+    )
     teacher_logits = lax.psum_scatter(
-        jnp.dot(rows_piece, teacher_head, preferred_element_type=jnp.float32).astype(jnp.bfloat16),
-        "tok",
-        scatter_dimension=0,
-        tiled=True,
+        teacher_part, "tok", scatter_dimension=0, tiled=True
     ).astype(jnp.float32)
-    rows_piece = student_all
-    student_logits = lax.psum_scatter(
-        jnp.dot(rows_piece, student_head, preferred_element_type=jnp.float32),
-        "tok",
-        scatter_dimension=0,
-        tiled=True,
-    )
     differ = student_logits - teacher_logits
     vocab_start = lax.axis_index("voc") * vocab_local
     picked = sampled_ids[:, None] - vocab_start == jnp.arange(vocab_local, dtype=jnp.int32)[None, :]
-    picked_s = jnp.sum(jnp.where(picked, student_logits, 0.0), axis=1)
-    picked_t = jnp.sum(jnp.where(picked, teacher_logits, 0.0), axis=1)
     local_tmax = jnp.max(teacher_logits, axis=1)
     local_smax = jnp.max(student_logits, axis=1)
-    teacher_max, student_max = lax.pmax((local_tmax, local_smax), "voc")
-    student_exp = jnp.exp(student_logits - student_max[:, None])
-    teacher_sum, student_sum, cross_sum, picked_s, picked_t = lax.psum(
-        (
-            jnp.sum(jnp.exp(teacher_logits - teacher_max[:, None]), axis=1),
+    student_exp = jnp.exp(student_logits - local_smax[:, None])
+    stats = jnp.stack(
+        [
+            local_tmax,
+            local_smax,
+            jnp.sum(jnp.exp(teacher_logits - local_tmax[:, None]), axis=1),
             jnp.sum(student_exp, axis=1),
             jnp.sum(student_exp * differ, axis=1),
-            picked_s,
-            picked_t,
-        ),
-        "voc",
-    )
+            jnp.sum(jnp.where(picked, student_logits, 0.0), axis=1),
+            jnp.sum(jnp.where(picked, teacher_logits, 0.0), axis=1),
+            jnp.zeros_like(local_tmax),
+        ]
+    )
+    every = voc_gather(stats, voc_count, 3)
+    teacher_max = jnp.max(every[:, 0], axis=0)
+    student_max = jnp.max(every[:, 1], axis=0)
+    teacher_scale = jnp.exp(every[:, 0] - teacher_max[None, :])
+    student_scale = jnp.exp(every[:, 1] - student_max[None, :])
+    teacher_sum = jnp.sum(every[:, 2] * teacher_scale, axis=0)
+    student_sum = jnp.sum(every[:, 3] * student_scale, axis=0)
+    cross_sum = jnp.sum(every[:, 4] * student_scale, axis=0)
+    picked_s = jnp.sum(every[:, 5], axis=0)
+    picked_t = jnp.sum(every[:, 6], axis=0)
     teacher_norm = teacher_max + jnp.log(teacher_sum)
     student_norm = student_max + jnp.log(student_sum)
     expect = cross_sum / student_sum

time: 613 us -> 458 us (0.75)
  waiting for transfers between devices: 406 us -> 225 us
  Pallas kernels: 0 us -> 44.1 us
  blocking collectives: 90.6 us -> 75.2 us
    reduce_scatter x2, waiting for transfers between devices: 158 us -> 58.3 us  [the longest x1 58.3 us: per_device(): lax.psum_scatter(teacher_part, 'tok', scatter_dimension=0, tiled=True)]
    all_gather x2 -> x0, waiting for transfers between devices: 54.9 us -> none  [the longest x1 37.4 us: per_device(): tok_rows = lax.all_gather(normed, 'voc', axis=0, tiled=True)]
    pallas_call x0 -> x3, Pallas kernels: none -> 44.1 us  [voc_gather(): pl.pallas_call(functools.partial(gather_kernel, n), out_shape=jax.ShapeDt...]
    pmax x1 -> x0, blocking collectives: 27 us -> none  [per_device(): teacher_max, student_max = lax.pmax((local_tmax, local_smax), 'voc')]
    psum x1 -> x0, blocking collectives: 24.5 us -> none  [per_device(): lax.psum((jnp.sum(jnp.exp(teacher_logits - teacher_max[:, None]), axis=1)...]
    all_to_all x0 -> x1, blocking collectives: none -> 22.8 us  [per_device(): lax.all_to_all(tok_rows, 'tok', split_axis=1, concat_axis=0, tiled=True)]
    all_gather x1, waiting for transfers between devices: 78.1 us -> 57 us  [per_device(): lax.all_gather(logit_grad, 'tok', axis=0, tiled=True)]
    all_to_all x1 -> x0, waiting for transfers between devices: 14.2 us -> none  [per_device(): lax.all_to_all(tok_rows, 'tok', split_axis=1, concat_axis=0, tiled=True)]
  transfers between devices with their start and end apart: 8 -> 5, of which waited for: 8 -> 4; matrix products, arithmetic and copies ran while one was open for 4% -> 9% of each run, Pallas kernels for 0% -> 4%
where the time goes in v1:
time: 458 us; the launch traced here: 454 us
  waiting for transfers between devices  225 us (49%)
  blocking collectives  75.2 us (16%)
  matrix products  47.3 us (10%)
  Pallas kernels  44.1 us (10%)
  local copies, waits for them, and re-layouts  23.9 us (5%)
  other arithmetic  17 us (4%)
  between operations  13.9 us (3%)
  starting transfers between devices  7.66 us (2%)
    reduce_scatter x1, waiting for transfers between devices, per_device(): lax.psum_scatter(grad_terms.astype(jnp.bfloat16), 'voc', scatter_dimensio...  71.5 us
    reduce_scatter x1, waiting for transfers between devices, per_device(): lax.psum_scatter(teacher_part, 'tok', scatter_dimension=0, tiled=True)  58.3 us
    all_gather x1, waiting for transfers between devices, per_device(): lax.all_gather(logit_grad, 'tok', axis=0, tiled=True)  57 us
    all_to_all x1, blocking collectives, per_device(): lax.all_to_all(outgoing, ('tok', 'voc'), split_axis=0, concat_axis=0, til...  52.5 us
    pallas_call x3, Pallas kernels, voc_gather(): pl.pallas_call(functools.partial(gather_kernel, n), out_shape=jax.ShapeDt...  44.1 us
    all_to_all x1, waiting for transfers between devices, per_device(): lax.all_to_all(partial_out, ('tok', 'voc'), split_axis=0, concat_axis=0,...  38 us
    all_to_all x1, blocking collectives, per_device(): lax.all_to_all(tok_rows, 'tok', split_axis=1, concat_axis=0, tiled=True)  22.8 us
    dot_general x1, matrix products, per_device(): jnp.dot(student_all, student_head, preferred_element_type=jnp.float32)  12.1 us
  transfers between devices with their start and end apart: 5, of which 4 were waited for; matrix products, arithmetic and copies ran while one was open for 9% of the time, Pallas kernels for 4%

profile of v1, /device:TPU:17, one launch (start us, length us, event | category | flops | bytes accessed | tf_op | source)
XLA Modules:
  0.0 454.0 jit_solution(395699384748671774)
XLA Ops:
  7.2 0.9 eq.20
  8.6 0.7 multiply_add_fusion
  9.4 2.3 convolution_convert_fusion.2
  11.7 2.5 reshape.81
  14.2 18.4 %shard_map.131 = bf16[16,64,512]{2,1,0:T(8,128)(2,1)} custom-call(bf16[64,512]{1,0:T(8,128)(2,1)} %x_ref.1), custom_call_target="tpu_custom_call" | custom-call | tf_op jit(solution)/shard_map/pallas_call | solution.py:70
  32.7 12.1 %fusion.16 = f32[1024,4864]{1,0:T(8,128)} fusion(bf16[1024,512]{1,0:T(8,128)(2,1)} %bitcast.49, bf16[512,4864]{1,0:T(8,128)(2,1)} %param.21), kind=kOutput, calls=%fused_computation.50 | convolution fusion | flops 5100273664 | bytes 25952256 | tf_op jit(solution)/shard_map/dot_general | solution.py:110
  44.8 5.1 %broadcast_in_dim.21 = bf16[64,2,2,4096]{3,2,1,0:T(2,128)(2,1)} broadcast(bf16[64,2,4096]{2,1,0:T(2,128)(2,1)} %reshape.81), dimensions={0,2,3} | broadcast | bytes 3145728 | tf_op jit(solution)/shard_map/broadcast_in_dim | solution.py:108
  49.9 52.5 %all_to_all.29 = bf16[128,2,4096]{2,1,0:T(2,128)(2,1)} all-to-all(bf16[128,2,4096]{2,1,0:T(2,128)(2,1)} %bitcast.45), channel_id=1, replica_groups=mesh['tok'=8,'voc'=16] {'tok','voc'}, dimensions={0} | all-to-all | bytes 4194304 | tf_op jit(solution)/shard_map/all_to_all | solution.py:113
  102.3 4.2 reshape.84
  106.5 3.9 fusion.17
  110.4 6.5 %convolution_convert_fusion.1 = bf16[256,4096]{1,0:T(8,128)(2,1)} fusion(bf16[384,4096]{1,0:T(8,128)(2,1)S(1)} %copy-done, bf16[256,4096]{1,0:T(8,128)(2,1)} %reshape.84, bf16[4096,384]{1,0:T(8,128)(2,1)} %param.16, f32[256,384]{1,0:T(8,128)S(1)} %fusion.17), kind=kOutput, calls=%fused_computation.1 | convolution fusion | flops 1612251136 | bytes 10878976 | tf_op jit(solution)/shard_map/dot_general | solution.py:119
  116.9 4.4 reshape.85
  121.3 7.1 %all-to-all-start.1 = ((bf16[128,2,4096]{2,1,0:T(2,128)(2,1)}), bf16[128,2,4096]{2,1,0:T(2,128)(2,1)S(1)}, u32[]{:S(2)}, u32[]{:S(2)}) async-start(bf16[128,2,4096]{2,1,0:T(2,128)(2,1)} %reshape.85), calls=%async_computation.1 | async-start | bytes 4194304 | tf_op jit(solution)/shard_map/all_to_all | solution.py:123
  128.9 38.0 %all-to-all-done.1 = bf16[128,2,4096]{2,1,0:T(2,128)(2,1)S(1)} async-done(((bf16[128,2,4096]{2,1,0:T(2,128)(2,1)}), bf16[128,2,4096]{2,1,0:T(2,128)(2,1)S(1)}, u32[]{:S(2)}, u32[]{:S(2)}) %all-to-all-start.1) | async-done | bytes 2097184 | tf_op jit(solution)/shard_map/all_to_all | solution.py:123
  167.0 4.1 convert_reduce_fusion
  171.1 2.7 reshape.88
  173.9 1.2 multiply_reduce_fusion.1
  175.1 0.7 multiply_convert_fusion.1.x_ref
  175.8 16.6 %shard_map.132 = bf16[16,8,4096]{2,1,0:T(8,128)(2,1)} custom-call(bf16[8,4096]{1,0:T(8,128)(2,1)} %multiply_convert_fusion.1.x_ref), custom_call_target="tpu_custom_call" | custom-call | tf_op jit(solution)/shard_map/pallas_call | solution.py:70
  192.4 1.6 copy.28
  194.3 22.8 %all_to_all.30 = bf16[128,8,512]{2,0,1:T(8,128)(2,1)S(1)} all-to-all(bf16[128,8,512]{2,0,1:T(8,128)(2,1)S(1)} %copy.21), channel_id=1, replica_groups=mesh['tok'=8,'voc'=16] {'tok'}, dimensions={1} | all-to-all | bytes 2097152 | tf_op jit(solution)/shard_map/all_to_all | solution.py:132
  217.1 10.2 %convolution_convert_fusion = bf16[1024,4864]{1,0:T(8,128)(2,1)} fusion(bf16[1024,512]{1,0:T(8,128)(2,1)S(1)} %bitcast.48, bf16[512,4864]{1,0:T(8,128)(2,1)} %param.19), kind=kOutput, calls=%fused_computation | convolution fusion | flops 5105254400 | bytes 15990784 | tf_op jit(solution)/shard_map/dot_general | solution.py:134
  227.9 1.1 copy-done.2
  229.2 58.3 %reduce-scatter.6.cloned.1.call-done = bf16[128,4864]{1,0:T(8,128)(2,1)} async-done(((bf16[1024,4864]{1,0:T(8,128)(2,1)}), bf16[128,4864]{1,0:T(8,128)(2,1)}) %reduce-scatter.6.cloned.1.call-update) | async-done | bytes 1245200 | tf_op jit(solution)/shard_map/reduce_scatter | solution.py:138
  287.5 1.5 reduce_max.45
  289.1 3.6 multiply_reduce_fusion
  293.3 9.1 %shard_map.133 = f32[16,8,128]{2,1,0:T(8,128)} custom-call(f32[8,128]{1,0:T(8,128)} %stack.28.x_ref), custom_call_target="tpu_custom_call" | custom-call | tf_op jit(solution)/shard_map/pallas_call | solution.py:70
  302.3 1.2 fusion.14
  304.2 3.5 multiply_convert_fusion
  307.8 57.0 %all-gather.2.cloned.1.call-done = bf16[1024,4864]{1,0:T(8,128)(2,1)} async-done(((bf16[128,4864]{1,0:T(8,128)(2,1)}), bf16[1024,4864]{1,0:T(8,128)(2,1)}) %all-gather.2.cloned.1.call-update) | async-done | bytes 9961488 | tf_op jit(solution)/shard_map/all_gather | solution.py:181
  364.7 11.1 %convolution_convert_fusion.3 = bf16[1024,512]{1,0:T(8,128)(2,1)} fusion(bf16[1024,4864]{1,0:T(8,128)(2,1)} %all-gather.2.cloned.1.call-done, bf16[512,4864]{1,0:T(8,128)(2,1)} %param.21), kind=kOutput, calls=%fused_computation.17 | convolution fusion | flops 5100797952 | bytes 15990784 | tf_op jit(solution)/shard_map/dot_general | solution.py:180
  375.9 71.5 %reduce-scatter.8.cloned.1.call-done = bf16[64,512]{1,0:T(8,128)(2,1)} async-done(((bf16[1024,512]{1,0:T(8,128)(2,1)}), bf16[64,512]{1,0:T(8,128)(2,1)}) %reduce-scatter.8.cloned.1.call-update) | async-done | bytes 65552 | tf_op jit(solution)/shard_map/reduce_scatter | solution.py:186
  (43 shorter events, 3.6 us)
Async XLA Ops:
  7.2 103.3 %copy-start = (bf16[384,4096]{1,0:T(8,128)(2,1)S(1)}, bf16[384,4096]{1,0:T(8,128)(2,1)}, u32[]{:S(2)}) copy-start(bf16[384,4096]{1,0:T(8,128)(2,1)} %param.17) | copy-start | bytes 9437188
  7.2 220.1 %reduce-scatter.4.cloned.1.call-start = ((), (), s32[]{:S(2)}) async-start(), calls=%async_computation.6 | async-start | bytes 22413312 | tf_op jit(solution)/shard_map/reduce_scatter | solution.py:112
  121.3 7.3 %copy-start.4 = (f32[8,8]{1,0:T(8,128)S(1)}, f32[8,8]{1,0:T(8,128)}, u32[]{:S(2)}) copy-start(f32[8,8]{1,0:T(8,128)} %param.13) | copy-start | bytes 772
  121.3 45.7 %all-to-all-start.1 = ((bf16[128,2,4096]{2,1,0:T(2,128)(2,1)}), bf16[128,2,4096]{2,1,0:T(2,128)(2,1)S(1)}, u32[]{:S(2)}, u32[]{:S(2)}) async-start(bf16[128,2,4096]{2,1,0:T(2,128)(2,1)} %reshape.85), calls=%async_computation.1 | async-start | bytes 4194304 | tf_op jit(solution)/shard_map/all_to_all | solution.py:123
  128.4 159.1 %reduce-scatter.6.cloned.1.call-start = ((), (), s32[]{:S(2)}) async-start(), calls=%async_computation.7 | async-start | bytes 11206656 | tf_op jit(solution)/shard_map/reduce_scatter | solution.py:138
  171.1 2.7 copy-start.3
  171.1 4.0 copy-start.5
  227.3 0.7 copy-start.7
  227.3 1.7 copy-start.2
  227.3 137.4 %all-gather.2.cloned.1.call-start = ((), (), s32[]{:S(2)}) async-start(), calls=%async_computation.8 | async-start | bytes 11206656 | tf_op jit(solution)/shard_map/all_gather | solution.py:181
  229.2 75.0 %copy-start.6 = (f32[128]{0:T(128)S(1)}, f32[128]{0:T(128)}, u32[]{:S(2)}) copy-start(f32[128]{0:T(128)} %param.23) | copy-start | bytes 1540
  307.7 139.7 %reduce-scatter.8.cloned.1.call-start = ((), (), s32[]{:S(2)}) async-start(), calls=%async_computation.9 | async-start | bytes 1114112 | tf_op jit(solution)/shard_map/reduce_scatter | solution.py:186
  364.7 82.7 %copy-start.1 = (bf16[384,4096]{1,0:T(8,128)(2,1)S(1)}, bf16[384,4096]{1,0:T(8,128)(2,1)}, u32[]{:S(2)}) copy-start(bf16[384,4096]{1,0:T(8,128)(2,1)} %param.17) | copy-start | bytes 9437188
Sparse Core Ops, SparseCore 0:
  50.0 155.4 reduce-scatter.3
  227.4 60.0 reduce-scatter.5
  307.8 56.8 all-gather.1
  376.0 71.3 reduce-scatter.7

commit v2 on v1

--- a/solution.py
+++ b/solution.py
@@ -79,6 +79,174 @@
         ],
         compiler_params=pltpu.CompilerParams(collective_id=collective_id, has_side_effects=True),
     )(x)
+
+
+def grad_kernel(
+    g_ref, own_hbm, pair_hbm, out_ref,
+    own_w, pair_w, blocks, terms, landed,
+    load_sem, ring_send, ring_recv, term_send, term_recv, self_sem,
+):
+    t, v = lax.axis_index("tok"), lax.axis_index("voc")
+    core = lax.rem(t, 2)
+    chip = t // 2
+    partner = t + 1 - 2 * core
+    right, left = lax.rem(t + 2, 8), lax.rem(t + 6, 8)
+    half = g_ref.shape[0] // 2
+    source_core = lax.rem(v // 2, 2)
+    loads = (
+        pltpu.make_async_copy(own_hbm, own_w, load_sem.at[0]),
+        pltpu.make_async_copy(pair_hbm, pair_w, load_sem.at[1]),
+    )
+    for load in loads:
+        load.start()
+
+    barrier = pltpu.get_barrier_semaphore()
+    for side in (right, left):
+        pl.semaphore_signal(barrier, inc=1, device_id=(side, v), device_id_type=MESH)
+
+    @pl.loop(0, 16)
+    def _(k):
+        @pl.when(jnp.logical_or(source_core != core, k != v))
+        def _():
+            pl.semaphore_signal(
+                barrier, inc=1, device_id=(chip * 2 + source_core, k), device_id_type=MESH
+            )
+
+    @pl.when(source_core == core)
+    def _():
+        pl.semaphore_wait(barrier, 17)
+
+    @pl.when(source_core != core)
+    def _():
+        pl.semaphore_wait(barrier, 18)
+
+    top, low = pl.ds(0, half), pl.ds(half, half)
+    plan = (
+        (g_ref.at[top], blocks.at[0, top], right),
+        (g_ref.at[low], blocks.at[0, low], right),
+        (g_ref.at[low], blocks.at[1, low], left),
+        (g_ref.at[top], blocks.at[1, top], left),
+        (blocks.at[0, top], blocks.at[2, top], right),
+        (blocks.at[1, low], blocks.at[2, low], left),
+    )
+    ring = [
+        pltpu.make_async_remote_copy(
+            src_ref=source,
+            dst_ref=target,
+            send_sem=ring_send.at[i],
+            recv_sem=ring_recv.at[i],
+            device_id=(device, v),
+            device_id_type=MESH,
+        )
+        for i, (source, target, device) in enumerate(plan)
+    ]
+    for i in (0, 2, 1, 3):
+        ring[i].start()
+    for load in loads:
+        load.wait()
+
+    def term_copy(slot, side, h, piece):
+        return pltpu.make_async_remote_copy(
+            src_ref=terms.at[slot, side, pl.ds(h * half, half)],
+            dst_ref=landed.at[v],
+            send_sem=term_send.at[slot * 4 + side * 2 + h],
+            recv_sem=term_recv.at[v],
+            device_id=(partner if side else t, piece),
+            device_id_type=MESH,
+        )
+
+    def self_copy(slot, h):
+        return pltpu.make_async_copy(
+            terms.at[slot, 0, pl.ds(h * half, half)], landed.at[v], self_sem
+        )
+
+    pieces = [
+        [lax.rem(chip + shift, 4) * 4 + 2 * core + h for h in range(2)] for shift in (0, 3, 1, 2)
+    ]
+
+    def multiply(slot, block):
+        for side, weight in enumerate((own_w, pair_w)):
+            terms[slot, side] = lax.dot_general(
+                block[...], weight[...], (((1,), (1,)), ((), ())), preferred_element_type=jnp.float32
+            ).astype(jnp.bfloat16)
+            for h in range(2):
+                piece = pieces[slot][h]
+                if side:
+                    term_copy(slot, side, h, piece).start()
+                else:
+                    pl.when(piece != v)(term_copy(slot, side, h, piece).start)
+                    pl.when(piece == v)(self_copy(slot, h).start)
+
+    multiply(0, g_ref)
+    ring[0].wait_recv()
+    ring[4].start()
+    ring[2].wait_recv()
+    ring[5].start()
+    ring[1].wait_recv()
+    multiply(1, blocks.at[0])
+    ring[3].wait_recv()
+    multiply(2, blocks.at[1])
+    ring[4].wait_recv()
+    ring[5].wait_recv()
+    multiply(3, blocks.at[2])
+
+    for slot in range(4):
+        for h in range(2):
+            piece = pieces[slot][h]
+            term_copy(slot, 1, h, piece).wait_send()
+            pl.when(piece != v)(term_copy(slot, 0, h, piece).wait_send)
+            pl.when(piece == v)(self_copy(slot, h).wait)
+    for copy in ring:
+        copy.wait_send()
+
+    @pl.loop(0, 16)
+    def _(k):
+        @pl.when(jnp.logical_or(source_core != core, k != v))
+        def _():
+            pltpu.make_async_remote_copy(
+                src_ref=terms.at[0, 0, top],
+                dst_ref=landed.at[k],
+                send_sem=term_send.at[0],
+                recv_sem=term_recv.at[k],
+                device_id=(partner, v),
+                device_id_type=MESH,
+            ).wait_recv()
+
+    total = landed[0].astype(jnp.float32)
+    for k in range(1, 16):
+        total += landed[k].astype(jnp.float32)
+    out_ref[...] = total.astype(out_ref.dtype)
+
+
+def grad_reduce(logit_grad, head_own, head_pair, collective_id):
+    rows, columns = logit_grad.shape
+    width = head_own.shape[0]
+    return pl.pallas_call(
+        grad_kernel,
+        out_shape=jax.ShapeDtypeStruct((rows // 2, width), jnp.bfloat16),
+        in_specs=[
+            pl.BlockSpec(memory_space=pltpu.VMEM),
+            pl.BlockSpec(memory_space=pl.ANY),
+            pl.BlockSpec(memory_space=pl.ANY),
+        ],
+        out_specs=pl.BlockSpec(memory_space=pltpu.VMEM),
+        scratch_shapes=[
+            pltpu.VMEM((width, columns), jnp.bfloat16),
+            pltpu.VMEM((width, columns), jnp.bfloat16),
+            pltpu.VMEM((3, rows, columns), jnp.bfloat16),
+            pltpu.VMEM((4, 2, rows, width), jnp.bfloat16),
+            pltpu.VMEM((16, rows // 2, width), jnp.bfloat16),
+            pltpu.SemaphoreType.DMA((2,)),
+            pltpu.SemaphoreType.DMA((6,)),
+            pltpu.SemaphoreType.DMA((6,)),
+            pltpu.SemaphoreType.DMA((16,)),
+            pltpu.SemaphoreType.DMA((16,)),
+            pltpu.SemaphoreType.DMA,
+        ],
+        compiler_params=pltpu.CompilerParams(
+            collective_id=collective_id, has_side_effects=True, vmem_limit_bytes=56 * 1024 * 1024
+        ),
+    )(logit_grad, head_own, head_pair)
 
 
 def per_device(
@@ -106,6 +274,7 @@
         jnp.bfloat16
     )
     outgoing = jnp.repeat(dispatched.reshape(experts, capacity, model_width), 2, axis=0)
+    student_pair = lax.ppermute(student_head, "tok", [(i, i ^ 1) for i in range(tok_count)])
     student_all = voc_gather(student_hidden, voc_count, 1).reshape(-1, student_hidden.shape[1])
     student_part = jnp.dot(student_all, student_head, preferred_element_type=jnp.float32)
     outgoing, student_part = lax.optimization_barrier((outgoing, student_part))
@@ -177,15 +346,7 @@
         token_weight[:, None]
         * (student_prob * (differ - expect[:, None]) + picked.astype(jnp.float32) - student_prob)
     ).astype(jnp.bfloat16)
-    grad_terms = lax.dot_general(
-        lax.all_gather(logit_grad, "tok", axis=0, tiled=True),
-        student_head,
-        (((1,), (1,)), ((), ())),
-        preferred_element_type=jnp.float32,
-    )
-    hidden_grad = lax.psum_scatter(
-        grad_terms.astype(jnp.bfloat16), "voc", scatter_dimension=0, tiled=True
-    )
+    hidden_grad = grad_reduce(logit_grad, student_head, student_pair, 4)
     return (token_loss, hidden_grad)
 
 

time: 458 us -> 382 us (0.83)
  waiting for transfers between devices: 225 us -> 96.4 us
  Pallas kernels: 44.1 us -> 109 us
  matrix products: 47.3 us -> 36.2 us
    reduce_scatter x1 -> x0, waiting for transfers between devices: 71.5 us -> none  [per_device(): lax.psum_scatter(grad_terms.astype(jnp.bfloat16), 'voc', scatter_dimensio...]
    pallas_call x0 -> x1, Pallas kernels: none -> 64.5 us  [grad_reduce(): pl.pallas_call(grad_kernel, out_shape=jax.ShapeDtypeStruct((rows // 2, wi...]
    all_gather x1 -> x0, waiting for transfers between devices: 57 us -> none  [per_device(): lax.all_gather(logit_grad, 'tok', axis=0, tiled=True)]
    dot_general x1 -> x0, matrix products: 11.1 us -> none  [per_device(): lax.dot_general(lax.all_gather(logit_grad, 'tok', axis=0, tiled=True), st...]
  transfers between devices with their start and end apart: 5 -> 4, of which waited for: 4 -> 2; matrix products, arithmetic and copies ran while one was open for 9% -> 14% of each run, Pallas kernels for 4% -> 7%
where the time goes in v2:
time: 382 us; the launch traced here: 380 us
  Pallas kernels  109 us (29%)
  waiting for transfers between devices  96.4 us (25%)
  blocking collectives  75.2 us (20%)
  matrix products  36.2 us (9%)
  local copies, waits for them, and re-layouts  24.3 us (6%)
  other arithmetic  17 us (4%)
  between operations  14.2 us (4%)
  starting transfers between devices  8.69 us (2%)
    pallas_call x1, Pallas kernels, grad_reduce(): pl.pallas_call(grad_kernel, out_shape=jax.ShapeDtypeStruct((rows // 2, wi...  64.5 us
    reduce_scatter x1, waiting for transfers between devices, per_device(): lax.psum_scatter(teacher_part, 'tok', scatter_dimension=0, tiled=True)  58.3 us
    all_to_all x1, blocking collectives, per_device(): lax.all_to_all(outgoing, ('tok', 'voc'), split_axis=0, concat_axis=0, til...  52.5 us
    pallas_call x3, Pallas kernels, voc_gather(): pl.pallas_call(functools.partial(gather_kernel, n), out_shape=jax.ShapeDt...  44.1 us
    all_to_all x1, waiting for transfers between devices, per_device(): lax.all_to_all(partial_out, ('tok', 'voc'), split_axis=0, concat_axis=0,...  38 us
    all_to_all x1, blocking collectives, per_device(): lax.all_to_all(tok_rows, 'tok', split_axis=1, concat_axis=0, tiled=True)  22.8 us
    dot_general x1, matrix products, per_device(): jnp.dot(student_all, student_head, preferred_element_type=jnp.float32)  12.1 us
    dot_general x1, matrix products, per_device(): jnp.dot(teacher_cols, teacher_head, preferred_element_type=jnp.float32)  10.2 us
  transfers between devices with their start and end apart: 4, of which 2 were waited for; matrix products, arithmetic and copies ran while one was open for 14% of the time, Pallas kernels for 7%

profile of v2, /device:TPU:17, one launch (start us, length us, event | category | flops | bytes accessed | tf_op | source)
XLA Modules:
  0.0 380.5 jit_solution(13708304305017354204)
XLA Ops:
  7.2 0.9 eq.20
  8.6 0.7 multiply_add_fusion
  9.4 2.3 convolution_convert_fusion.2
  11.7 2.5 reshape.81
  14.2 18.4 %shard_map.131 = bf16[16,64,512]{2,1,0:T(8,128)(2,1)} custom-call(bf16[64,512]{1,0:T(8,128)(2,1)} %x_ref.1), custom_call_target="tpu_custom_call" | custom-call | tf_op jit(solution)/shard_map/pallas_call | solution.py:70
  32.7 12.1 %fusion.16 = f32[1024,4864]{1,0:T(8,128)} fusion(bf16[1024,512]{1,0:T(8,128)(2,1)} %bitcast.47, bf16[512,4864]{1,0:T(8,128)(2,1)} %own_hbm.1), kind=kOutput, calls=%fused_computation.49 | convolution fusion | flops 5100273664 | bytes 25952256 | tf_op jit(solution)/shard_map/dot_general | solution.py:279
  44.8 5.1 %broadcast_in_dim.21 = bf16[64,2,2,4096]{3,2,1,0:T(2,128)(2,1)} broadcast(bf16[64,2,4096]{2,1,0:T(2,128)(2,1)} %reshape.81), dimensions={0,2,3} | broadcast | bytes 3145728 | tf_op jit(solution)/shard_map/broadcast_in_dim | solution.py:276
  49.9 52.5 %all_to_all.29 = bf16[128,2,4096]{2,1,0:T(2,128)(2,1)} all-to-all(bf16[128,2,4096]{2,1,0:T(2,128)(2,1)} %bitcast.43), channel_id=1, replica_groups=mesh['tok'=8,'voc'=16] {'tok','voc'}, dimensions={0} | all-to-all | bytes 4194304 | tf_op jit(solution)/shard_map/all_to_all | solution.py:282
  102.3 4.2 %reshape.84 = bf16[256,4096]{1,0:T(8,128)(2,1)} reshape(bf16[128,2,4096]{2,1,0:T(2,128)(2,1)} %all_to_all.29) | data formatting | bytes 4194304 | tf_op jit(solution)/shard_map/reshape | solution.py:283
  106.5 3.9 %fusion.17 = f32[256,384]{1,0:T(8,128)S(1)} fusion(bf16[256,4096]{1,0:T(8,128)(2,1)} %reshape.84, bf16[4096,384]{1,0:T(8,128)(2,1)} %param.15), kind=kOutput, calls=%fused_computation.50 | convolution fusion | flops 805306368 | bytes 5636096 | tf_op jit(solution)/shard_map/dot_general | solution.py:284
  110.4 6.5 %convolution_convert_fusion.1 = bf16[256,4096]{1,0:T(8,128)(2,1)} fusion(bf16[384,4096]{1,0:T(8,128)(2,1)S(1)} %copy-done, bf16[256,4096]{1,0:T(8,128)(2,1)} %reshape.84, bf16[4096,384]{1,0:T(8,128)(2,1)} %param.16, f32[256,384]{1,0:T(8,128)S(1)} %fusion.17), kind=kOutput, calls=%fused_computation.1 | convolution fusion | flops 1612251136 | bytes 10878976 | tf_op jit(solution)/shard_map/dot_general | solution.py:288
  116.9 4.4 %reshape.85 = bf16[128,2,4096]{2,1,0:T(2,128)(2,1)} reshape(bf16[256,4096]{1,0:T(8,128)(2,1)} %convolution_convert_fusion.1) | data formatting | bytes 4194304 | tf_op jit(solution)/shard_map/reshape | solution.py:290
  121.3 7.1 %all-to-all-start.1 = ((bf16[128,2,4096]{2,1,0:T(2,128)(2,1)}), bf16[128,2,4096]{2,1,0:T(2,128)(2,1)S(1)}, u32[]{:S(2)}, u32[]{:S(2)}) async-start(bf16[128,2,4096]{2,1,0:T(2,128)(2,1)} %reshape.85), calls=%async_computation.1 | async-start | bytes 4194304 | tf_op jit(solution)/shard_map/all_to_all | solution.py:292
  128.9 38.0 %all-to-all-done.1 = bf16[128,2,4096]{2,1,0:T(2,128)(2,1)S(1)} async-done(((bf16[128,2,4096]{2,1,0:T(2,128)(2,1)}), bf16[128,2,4096]{2,1,0:T(2,128)(2,1)S(1)}, u32[]{:S(2)}, u32[]{:S(2)}) %all-to-all-start.1) | async-done | bytes 2097184 | tf_op jit(solution)/shard_map/all_to_all | solution.py:292
  167.0 4.1 %convert_reduce_fusion = f32[64,2,4096]{2,1,0:T(2,128)} fusion(bf16[128,2,4096]{2,1,0:T(2,128)(2,1)S(1)} %all-to-all-done.1), kind=kLoop, calls=%fused_computation.4 | loop fusion | flops 1572864 | bytes 4194304 | tf_op jit(solution)/shard_map/reduce_sum | solution.py:293
  171.1 2.7 reshape.88
  173.9 1.2 multiply_reduce_fusion.1
  175.1 0.7 multiply_convert_fusion.1.x_ref
  175.8 16.6 %shard_map.132 = bf16[16,8,4096]{2,1,0:T(8,128)(2,1)} custom-call(bf16[8,4096]{1,0:T(8,128)(2,1)} %multiply_convert_fusion.1.x_ref), custom_call_target="tpu_custom_call" | custom-call | tf_op jit(solution)/shard_map/pallas_call | solution.py:70
  192.4 1.6 copy.28
  194.3 22.8 %all_to_all.30 = bf16[128,8,512]{2,0,1:T(8,128)(2,1)S(1)} all-to-all(bf16[128,8,512]{2,0,1:T(8,128)(2,1)S(1)} %copy.21), channel_id=1, replica_groups=mesh['tok'=8,'voc'=16] {'tok'}, dimensions={1} | all-to-all | bytes 2097152 | tf_op jit(solution)/shard_map/all_to_all | solution.py:301
  217.1 10.2 %convolution_convert_fusion = bf16[1024,4864]{1,0:T(8,128)(2,1)} fusion(bf16[1024,512]{1,0:T(8,128)(2,1)S(1)} %bitcast.46, bf16[512,4864]{1,0:T(8,128)(2,1)} %param.19), kind=kOutput, calls=%fused_computation | convolution fusion | flops 5105254400 | bytes 15990784 | tf_op jit(solution)/shard_map/dot_general | solution.py:303
  227.3 1.3 collective-permute-start
  229.2 58.3 %reduce-scatter.5.cloned.1.call-done = bf16[128,4864]{1,0:T(8,128)(2,1)} async-done(((bf16[1024,4864]{1,0:T(8,128)(2,1)}), bf16[128,4864]{1,0:T(8,128)(2,1)}) %reduce-scatter.5.cloned.1.call-update) | async-done | bytes 1245200 | tf_op jit(solution)/shard_map/reduce_scatter | solution.py:307
  287.5 1.5 reduce_max.45
  289.1 3.6 multiply_reduce_fusion
  292.7 0.6 stack.28.x_ref
  293.3 9.1 %shard_map.133 = f32[16,8,128]{2,1,0:T(8,128)} custom-call(f32[8,128]{1,0:T(8,128)} %stack.28.x_ref), custom_call_target="tpu_custom_call" | custom-call | tf_op jit(solution)/shard_map/pallas_call | solution.py:70
  302.3 1.2 fusion.14
  304.2 3.6 multiply_convert_fusion.g_ref
  307.7 64.5 %shard_map.134 = bf16[64,512]{1,0:T(8,128)(2,1)} custom-call(bf16[128,4864]{1,0:T(8,128)(2,1)} %multiply_convert_fusion.g_ref, bf16[512,4864]{1,0:T(8,128)(2,1)} %own_hbm.1, bf16[512,4864]{1,0:T(8,128)(2,1)} %collective-permute-done.pair_hbm), custom_call_target="tpu_custom_call" | custom-call | tf_op jit(solution)/shard_map/pallas_call | solution.py:224
  372.2 1.5 copy.30
  (40 shorter events, 2.6 us)
Async XLA Ops:
  7.2 103.3 %copy-start = (bf16[384,4096]{1,0:T(8,128)(2,1)S(1)}, bf16[384,4096]{1,0:T(8,128)(2,1)}, u32[]{:S(2)}) copy-start(bf16[384,4096]{1,0:T(8,128)(2,1)} %param.17) | copy-start | bytes 9437188
  7.2 220.1 %reduce-scatter.3.cloned.1.call-start = ((), (), s32[]{:S(2)}) async-start(), calls=%async_computation.5 | async-start | bytes 22413312 | tf_op jit(solution)/shard_map/reduce_scatter | solution.py:281
  121.3 7.3 %copy-start.4 = (f32[8,8]{1,0:T(8,128)S(1)}, f32[8,8]{1,0:T(8,128)}, u32[]{:S(2)}) copy-start(f32[8,8]{1,0:T(8,128)} %param.13) | copy-start | bytes 772
  121.3 45.7 %all-to-all-start.1 = ((bf16[128,2,4096]{2,1,0:T(2,128)(2,1)}), bf16[128,2,4096]{2,1,0:T(2,128)(2,1)S(1)}, u32[]{:S(2)}, u32[]{:S(2)}) async-start(bf16[128,2,4096]{2,1,0:T(2,128)(2,1)} %reshape.85), calls=%async_computation.1 | async-start | bytes 4194304 | tf_op jit(solution)/shard_map/all_to_all | solution.py:292
  128.4 159.1 %reduce-scatter.5.cloned.1.call-start = ((), (), s32[]{:S(2)}) async-start(), calls=%async_computation.6 | async-start | bytes 11206656 | tf_op jit(solution)/shard_map/reduce_scatter | solution.py:307
  171.1 2.7 copy-start.3
  171.1 4.0 %copy-start.5 = (f32[4096]{0:T(1024)S(1)}, f32[4096]{0:T(1024)}, u32[]{:S(2)}) copy-start(f32[4096]{0:T(1024)} %param.18) | copy-start | bytes 49156
  227.3 1.4 copy-start.7
  227.3 1.7 copy-start.2
  227.3 80.4 %collective-permute-start = (bf16[512,4864]{1,0:T(8,128)(2,1)}, bf16[512,4864]{1,0:T(8,128)(2,1)}, u32[]{:S(2)}, u32[]{:S(2)}) collective-permute-start(bf16[512,4864]{1,0:T(8,128)(2,1)} %own_hbm.1), channel_id=1, source_target_pairs={{0,16},{16,0},{32,48},{48,32},{64,80},{80,64},{96,112},{112,96},{1... | collective-permute-start | bytes 14942216 | tf_op jit(solution)/shard_map/ppermute | solution.py:277
  229.2 75.0 %copy-start.6 = (f32[128]{0:T(128)S(1)}, f32[128]{0:T(128)}, u32[]{:S(2)}) copy-start(f32[128]{0:T(128)} %param.23) | copy-start | bytes 1540
  307.7 65.9 %copy-start.1 = (bf16[384,4096]{1,0:T(8,128)(2,1)S(1)}, bf16[384,4096]{1,0:T(8,128)(2,1)}, u32[]{:S(2)}) copy-start(bf16[384,4096]{1,0:T(8,128)(2,1)} %param.17) | copy-start | bytes 9437188
Sparse Core Ops, SparseCore 0:
  50.0 155.4 reduce-scatter.2
  227.4 60.0 reduce-scatter.4

commit v3 on v2

--- a/solution.py
+++ b/solution.py
@@ -9,76 +9,93 @@
 MESH = pl.DeviceIdType.MESH
 
 
-def route_tables(expert_ids, gate_raw, experts, capacity):
-    rows_here, top_k = expert_ids.shape
-    flat_ids = expert_ids.reshape(-1)
-    one_hot = (flat_ids[:, None] == jnp.arange(experts, dtype=jnp.int32)[None, :]).astype(jnp.int32)
-    earlier = jnp.cumsum(one_hot, axis=0, dtype=jnp.int32) - one_hot
-    slot_of = jnp.sum(earlier * one_hot, axis=1, dtype=jnp.int32)
-    where_to = (flat_ids * capacity + slot_of).reshape(rows_here, top_k)
-    columns = jnp.arange(experts * capacity, dtype=jnp.int32)
-    matched = where_to[:, :, None] == columns[None, None, :]
-    shares = gate_raw / jnp.sum(gate_raw, axis=1, keepdims=True)
-    combine_table = jnp.sum(jnp.where(matched, shares[:, :, None], 0.0), axis=1)
-    dispatch_table = jnp.transpose(jnp.any(matched, axis=1)).astype(jnp.bfloat16)
-    return (dispatch_table, combine_table)
-
-
-def gather_kernel(n, x_ref, out_ref, send_sem, recv_sem, own_sem):
-    t, me = lax.axis_index("tok"), lax.axis_index("voc")
+def exchange_kernel(axis, n, count, source, target, *refs):
+    ins, outs = refs[:count], refs[count : 2 * count]
+    send_sem, recv_sem, own_sem = refs[2 * count :]
+    me = lax.axis_index(axis)
+
+    def device(k):
+        peer = lax.rem(me + k, n)
+        if axis == "tok":
+            return (peer, lax.axis_index("voc"))
+        return (lax.axis_index("tok"), peer)
+
     barrier = pltpu.get_barrier_semaphore()
 
     @pl.loop(1, n)
     def _(k):
-        pl.semaphore_signal(
-            barrier, inc=1, device_id=(t, lax.rem(me + k, n)), device_id_type=MESH
-        )
+        pl.semaphore_signal(barrier, inc=1, device_id=device(k), device_id_type=MESH)
 
     pl.semaphore_wait(barrier, n - 1)
 
-    def copy(k):
+    def copy(i, k, sender):
         return pltpu.make_async_remote_copy(
-            src_ref=x_ref,
-            dst_ref=out_ref.at[me],
-            send_sem=send_sem.at[k],
-            recv_sem=recv_sem.at[k],
-            device_id=(t, lax.rem(me + k, n)),
+            src_ref=source(ins[i], lax.rem(me + k, n)),
+            dst_ref=target(outs[i], sender),
+            send_sem=send_sem.at[i, k],
+            recv_sem=recv_sem.at[i, k],
+            device_id=device(k),
             device_id_type=MESH,
         )
 
-    @pl.loop(1, n)
-    def _(k):
-        copy(k).start()
-
-    own = pltpu.make_async_copy(x_ref, out_ref.at[me], own_sem)
-    own.start()
-    own.wait()
-
-    @pl.loop(1, n)
-    def _(k):
-        pltpu.make_async_remote_copy(
-            src_ref=x_ref,
-            dst_ref=out_ref.at[lax.rem(me - k + n, n)],
-            send_sem=send_sem.at[k],
-            recv_sem=recv_sem.at[k],
-            device_id=(t, lax.rem(me + k, n)),
-            device_id_type=MESH,
-        ).wait()
-
-
-def voc_gather(x, n, collective_id):
+    for i in range(count):
+
+        @pl.loop(1, n)
+        def _(k):
+            copy(i, k, me).start()
+
+    for i in range(count):
+        own = pltpu.make_async_copy(source(ins[i], me), target(outs[i], me), own_sem)
+        own.start()
+        own.wait()
+
+    for i in range(count):
+
+        @pl.loop(1, n)
+        def _(k):
+            copy(i, k, lax.rem(me - k + n, n)).wait()
+
+
+def whole(ref, peer):
+    return ref
+
+
+def at_peer(ref, peer):
+    return ref.at[peer]
+
+
+def at_pair(ref, peer):
+    return ref.at[peer // 2]
+
+
+def at_second(ref, peer):
+    return ref.at[:, peer]
+
+
+def at_core_chip(ref, peer):
+    return ref.at[lax.rem(peer, 2) * 4 + peer // 2]
+
+
+def at_core_features(ref, peer):
+    rows = pl.ds(pl.multiple_of(lax.rem(peer, 2) * 32, 32), 32)
+    return ref.at[rows, pl.ds(pl.multiple_of((peer // 2) * 1024, 1024), 1024)]
+
+
+def exchange(arrays, shapes, axis, collective_id, source=whole, target=at_peer):
+    n = lax.axis_size(axis)
+    count = len(arrays)
     return pl.pallas_call(
-        functools.partial(gather_kernel, n),
-        out_shape=jax.ShapeDtypeStruct((n,) + x.shape, x.dtype),
-        in_specs=[pl.BlockSpec(memory_space=pltpu.VMEM)],
-        out_specs=pl.BlockSpec(memory_space=pltpu.VMEM),
+        functools.partial(exchange_kernel, axis, n, count, source, target),
+        out_shape=[jax.ShapeDtypeStruct(o, x.dtype) for o, x in zip(shapes, arrays)],
+        in_specs=[pl.BlockSpec(memory_space=pltpu.VMEM)] * count,
+        out_specs=[pl.BlockSpec(memory_space=pltpu.VMEM)] * count,
         scratch_shapes=[
-            pltpu.SemaphoreType.DMA((n,)),
-            pltpu.SemaphoreType.DMA((n,)),
+            pltpu.SemaphoreType.DMA((count, n)),
+            pltpu.SemaphoreType.DMA((count, n)),
             pltpu.SemaphoreType.DMA,
         ],
         compiler_params=pltpu.CompilerParams(collective_id=collective_id, has_side_effects=True),
-    )(x)
+    )(*arrays)
 
 
 def grad_kernel(
@@ -249,6 +266,170 @@
     )(logit_grad, head_own, head_pair)
 
 
+def head_kernel(
+    rows_ref, squares_ref, own_hbm, pair_hbm, out_ref,
+    own_w, pair_w, far, kept, relay, sent, final, squares,
+    load_sem, ring_send, ring_recv, square_send, square_recv,
+):
+    t, v = lax.axis_index("tok"), lax.axis_index("voc")
+    core = lax.rem(t, 2)
+    chip = t // 2
+    right, left, across = lax.rem(t + 2, 8), lax.rem(t + 6, 8), lax.rem(t + 4, 8)
+    half = rows_ref.shape[1] // 2
+    width = own_w.shape[0]
+    features = rows_ref.shape[2] * 4
+    loads = (
+        pltpu.make_async_copy(own_hbm, own_w, load_sem.at[0]),
+        pltpu.make_async_copy(pair_hbm, pair_w, load_sem.at[1]),
+    )
+    for load in loads:
+        load.start()
+    barrier = pltpu.get_barrier_semaphore()
+    for side in (right, left, across):
+        pl.semaphore_signal(barrier, inc=1, device_id=(side, v), device_id_type=MESH)
+    pl.semaphore_wait(barrier, 3)
+
+    chips = [lax.rem(chip + shift, 4) for shift in range(4)]
+    square_copies = [
+        pltpu.make_async_remote_copy(
+            src_ref=squares_ref.at[chips[shift]],
+            dst_ref=squares.at[shift - 1],
+            send_sem=square_send.at[shift - 1],
+            recv_sem=square_recv.at[shift - 1],
+            device_id=(device, v),
+            device_id_type=MESH,
+        )
+        for shift, device in ((1, right), (2, across), (3, left))
+    ]
+    top, low = pl.ds(0, half), pl.ds(half, half)
+    plan = (
+        (far.at[top], relay.at[0], right),
+        (far.at[low], relay.at[1], left),
+        (sent.at[0, low], final.at[0, low], right),
+        (sent.at[1, top], final.at[1, top], left),
+        (sent.at[0, top], final.at[0, top], right),
+        (sent.at[1, low], final.at[1, low], left),
+    )
+    ring = [
+        pltpu.make_async_remote_copy(
+            src_ref=source,
+            dst_ref=target,
+            send_sem=ring_send.at[i],
+            recv_sem=ring_recv.at[i],
+            device_id=(device, v),
+            device_id_type=MESH,
+        )
+        for i, (source, target, device) in enumerate(plan)
+    ]
+    own_columns = pl.ds(pl.multiple_of(core * width, width), width)
+    pair_columns = pl.ds(pl.multiple_of((1 - core) * width, width), width)
+    step = 256
+    steps = own_w.shape[1] // step
+
+    def multiply(shift, store):
+        own_rows = rows_ref[chips[shift], :, own_columns]
+        pair_rows = rows_ref[chips[shift], :, pair_columns]
+
+        @pl.loop(0, steps)
+        def _(j):
+            columns = pl.ds(pl.multiple_of(j * step, step), step)
+            store(
+                columns,
+                jnp.dot(own_rows, own_w[:, columns], preferred_element_type=jnp.float32)
+                + jnp.dot(pair_rows, pair_w[:, columns], preferred_element_type=jnp.float32),
+            )
+
+    def store_far(columns, value):
+        far[:, columns] = value.astype(jnp.bfloat16)
+
+    def store_right(columns, value):
+        kept[0, :, columns] = value[:half]
+        sent[0, low, columns] = value[half:].astype(jnp.bfloat16)
+
+    def store_left(columns, value):
+        kept[1, :, columns] = value[half:]
+        sent[1, top, columns] = value[:half].astype(jnp.bfloat16)
+
+    def store_own(columns, value):
+        out_ref[:, columns] = value
+
+    for load in loads:
+        load.wait()
+    multiply(2, store_far)
+    ring[0].start()
+    ring[1].start()
+    multiply(1, store_right)
+    ring[2].start()
+    multiply(3, store_left)
+    ring[3].start()
+    for copy in square_copies:
+        copy.start()
+    multiply(0, store_own)
+    for i, rows in ((0, top), (1, low)):
+        ring[i].wait_recv()
+
+        @pl.loop(0, steps)
+        def _(j):
+            columns = pl.ds(pl.multiple_of(j * step, step), step)
+            sent[i, rows, columns] = (
+                kept[i, :, columns] + relay[i, :, columns].astype(jnp.float32)
+            ).astype(jnp.bfloat16)
+
+        ring[4 + i].start()
+    total = squares_ref[chip]
+    for i, copy in enumerate(square_copies):
+        copy.wait_recv()
+        total += squares[i]
+    inverse = lax.rsqrt(total[:, :1] / features + 1e-06)
+    for i in range(2, 6):
+        ring[i].wait_recv()
+
+    @pl.loop(0, steps)
+    def _(j):
+        columns = pl.ds(pl.multiple_of(j * step, step), step)
+        out_ref[:, columns] = (
+            out_ref[:, columns]
+            + final[0, :, columns].astype(jnp.float32)
+            + final[1, :, columns].astype(jnp.float32)
+        ) * inverse
+
+    for copy in square_copies:
+        copy.wait_send()
+    for copy in ring:
+        copy.wait_send()
+
+
+def head_reduce(rows, squares, head_own, head_pair, collective_id):
+    chips, count, _ = rows.shape
+    width, columns = head_own.shape
+    vmem = pl.BlockSpec(memory_space=pltpu.VMEM)
+    hbm = pl.BlockSpec(memory_space=pl.ANY)
+    return pl.pallas_call(
+        head_kernel,
+        out_shape=jax.ShapeDtypeStruct((count, columns), jnp.float32),
+        in_specs=[vmem, vmem, hbm, hbm],
+        out_specs=vmem,
+        scratch_shapes=[
+            pltpu.VMEM((width, columns), jnp.bfloat16),
+            pltpu.VMEM((width, columns), jnp.bfloat16),
+            pltpu.VMEM((count, columns), jnp.bfloat16),
+            pltpu.VMEM((2, count // 2, columns), jnp.float32),
+            pltpu.VMEM((2, count // 2, columns), jnp.bfloat16),
+            pltpu.VMEM((2, count, columns), jnp.bfloat16),
+            pltpu.VMEM((2, count, columns), jnp.bfloat16),
+            pltpu.VMEM((3, count, 128), jnp.float32),
+            pltpu.SemaphoreType.DMA((2,)),
+            pltpu.SemaphoreType.DMA((6,)),
+            pltpu.SemaphoreType.DMA((6,)),
+            pltpu.SemaphoreType.DMA((3,)),
+            pltpu.SemaphoreType.DMA((3,)),
+        ],
+        compiler_params=pltpu.CompilerParams(
+            collective_id=collective_id, has_side_effects=True, vmem_limit_bytes=56 * 1024 * 1024
+        ),
+    )(rows, squares, head_own, head_pair)
+
+
 def per_device(
     tokens_in,
     gate_raw,
@@ -265,48 +446,120 @@
 ):
     tok_count = lax.axis_size("tok")
     voc_count = lax.axis_size("voc")
-    experts = tok_count * voc_count // 2
     rows_here, top_k = expert_ids.shape
     model_width = tokens_in.shape[1]
-    capacity = max(2, 2 * rows_here * top_k // experts)
-    dispatch_table, combine_table = route_tables(expert_ids, gate_raw, experts, capacity)
-    dispatched = jnp.dot(dispatch_table, tokens_in, preferred_element_type=jnp.float32).astype(
-        jnp.bfloat16
-    )
-    outgoing = jnp.repeat(dispatched.reshape(experts, capacity, model_width), 2, axis=0)
+    part_width = model_width // tok_count
     student_pair = lax.ppermute(student_head, "tok", [(i, i ^ 1) for i in range(tok_count)])
-    student_all = voc_gather(student_hidden, voc_count, 1).reshape(-1, student_hidden.shape[1])
+    teacher_pair = lax.ppermute(teacher_head, "tok", [(i, i ^ 1) for i in range(tok_count)])
+    student_all = lax.all_gather(student_hidden, "voc", axis=0, tiled=True)
     student_part = jnp.dot(student_all, student_head, preferred_element_type=jnp.float32)
-    outgoing, student_part = lax.optimization_barrier((outgoing, student_part))
+    ids_shares = jnp.concatenate(
+        [expert_ids.astype(jnp.float32), gate_raw, jnp.zeros((rows_here, 128 - 2 * top_k), jnp.float32)],
+        axis=1,
+    )
+    rows_all = tok_count * rows_here
+    tokens_all, table = exchange(
+        [tokens_in, ids_shares],
+        [(tok_count, rows_here, model_width), (tok_count, rows_here, 128)],
+        "tok",
+        2,
+        target=at_core_chip,
+    )
+    tokens_all = tokens_all.reshape(rows_all, model_width)
+    table = table.reshape(rows_all, 128)
+    slots = 2
+    here = voc_count // 2
+    column = jnp.arange(here * tok_count * slots, dtype=jnp.int32)
+    column_expert = column // (tok_count * slots) + lax.axis_index("tok") * here
+    column_block = column // slots % tok_count
+    column_slot = column % slots
+    row = jnp.arange(rows_all, dtype=jnp.int32)
+    gates = table[:, top_k : 2 * top_k]
+    shares = gates / jnp.sum(gates, axis=1, keepdims=True)
+    named = [
+        table[:, k : k + 1] == column_expert.astype(jnp.float32)[None, :] for k in range(top_k)
+    ]
+    present = functools.reduce(jnp.logical_or, named)
+    share_of = sum(jnp.where(named[k], shares[:, k : k + 1], 0.0) for k in range(top_k))
+    before = (row[:, None] // rows_here == row[None, :] // rows_here) & (row[None, :] < row[:, None])
+    earlier = jnp.dot(
+        before.astype(jnp.bfloat16), present.astype(jnp.bfloat16), preferred_element_type=jnp.float32
+    )
+    matched = (
+        present
+        & (earlier == column_slot.astype(jnp.float32)[None, :])
+        & (row[:, None] // rows_here == column_block[None, :])
+    )
+    combine_table = jnp.where(matched, share_of, 0.0)
+    dispatched = lax.dot_general(
+        matched.astype(jnp.bfloat16),
+        tokens_all,
+        (((0,), (0,)), ((), ())),
+        preferred_element_type=jnp.float32,
+    ).astype(jnp.bfloat16)
+    group = tok_count * slots
+    (arrived,) = exchange(
+        [dispatched.reshape(here, group, model_width)],
+        [(voc_count, group, model_width)],
+        "voc",
+        3,
+        source=at_pair,
+    )
+    arrived, student_part = lax.optimization_barrier((arrived, student_part))
     student_logits = lax.psum_scatter(student_part, "tok", scatter_dimension=0, tiled=True)
-    arrived = lax.all_to_all(outgoing, ("tok", "voc"), split_axis=0, concat_axis=0, tiled=True)
-    expert_rows = arrived.reshape(2 * experts * capacity, model_width)
+    expert_rows = arrived.reshape(voc_count * group, model_width)
     gate_part = jnp.dot(expert_rows, w_gate, preferred_element_type=jnp.float32)
     up_part = jnp.dot(expert_rows, w_up, preferred_element_type=jnp.float32)
     hidden_units = (jax.nn.silu(gate_part) * up_part).astype(jnp.bfloat16)
-    partial_out = (
-        jnp.dot(hidden_units, w_down, preferred_element_type=jnp.float32)
-        .astype(jnp.bfloat16)
-        .reshape(2 * experts, capacity, model_width)
-    )
-    returned = lax.all_to_all(partial_out, ("tok", "voc"), split_axis=0, concat_axis=0, tiled=True)
+    partial_out = jnp.dot(hidden_units, w_down, preferred_element_type=jnp.float32).astype(
+        jnp.bfloat16
+    )
+    (returned,) = exchange(
+        [partial_out.reshape(voc_count, group, model_width)],
+        [(voc_count, group, model_width)],
+        "voc",
+        5,
+        source=at_peer,
+    )
     pair_sum = jnp.sum(
-        returned.astype(jnp.float32).reshape(experts, 2, capacity, model_width), axis=1
-    ).reshape(experts * capacity, model_width)
-    expert_mix = jnp.dot(combine_table, pair_sum, precision=lax.Precision.HIGHEST)
-    residual_sum = tokens_in.astype(jnp.float32) + expert_mix
-    inverse = lax.rsqrt(jnp.mean(residual_sum * residual_sum, axis=1, keepdims=True) + 1e-06)
-    normed = (residual_sum * inverse * final_gain[None, :]).astype(jnp.bfloat16)
-    tok_rows = voc_gather(normed, voc_count, 2).reshape(-1, model_width)
-    teacher_cols = lax.all_to_all(tok_rows, "tok", split_axis=1, concat_axis=0, tiled=True)
+        returned.astype(jnp.float32).reshape(here, 2, group, model_width), axis=1
+    ).reshape(here * group, model_width)
+    mix_part = jnp.dot(combine_table, pair_sum, precision=lax.Precision.HIGHEST)
+    core_rows, chip_width = rows_all // 2, 2 * part_width
+    (mix_parts,) = exchange(
+        [mix_part], [(tok_count, core_rows, chip_width)], "tok", 6, source=at_core_features
+    )
+    tok_index = lax.axis_index("tok")
+    feature_start = (tok_index // 2) * chip_width
+    tokens_part = lax.dynamic_slice(
+        tokens_all, ((tok_index % 2) * core_rows, feature_start), (core_rows, chip_width)
+    )
+    residual_sum = tokens_part.astype(jnp.float32) + jnp.sum(mix_parts, axis=0)
+    squares = jnp.sum(residual_sum * residual_sum, axis=1, keepdims=True)
+    gain_part = lax.dynamic_slice_in_dim(final_gain, feature_start, chip_width, 0)
+    scaled = (residual_sum * gain_part[None, :]).astype(jnp.bfloat16)
+    chips = tok_count // 2
+    teacher_rows, squares_rows = exchange(
+        [
+            scaled.reshape(chips, rows_here, chip_width),
+            jnp.broadcast_to(squares, (core_rows, 128)).reshape(chips, rows_here, 128),
+        ],
+        [
+            (chips, voc_count, rows_here, chip_width),
+            (chips, voc_count, rows_here, 128),
+        ],
+        "voc",
+        8,
+        target=at_second,
+    )
     vocab_local = teacher_head.shape[1]
-    teacher_part = jnp.dot(teacher_cols, teacher_head, preferred_element_type=jnp.float32)
-    teacher_part, student_logits = lax.optimization_barrier(
-        (teacher_part.astype(jnp.bfloat16), student_logits)
-    )
-    teacher_logits = lax.psum_scatter(
-        teacher_part, "tok", scatter_dimension=0, tiled=True
-    ).astype(jnp.float32)
+    teacher_logits = head_reduce(
+        teacher_rows.reshape(chips, voc_count * rows_here, chip_width),
+        squares_rows.reshape(chips, voc_count * rows_here, 128),
+        teacher_head,
+        teacher_pair,
+        10,
+    )
     differ = student_logits - teacher_logits
     vocab_start = lax.axis_index("voc") * vocab_local
     picked = sampled_ids[:, None] - vocab_start == jnp.arange(vocab_local, dtype=jnp.int32)[None, :]
@@ -325,7 +578,7 @@
             jnp.zeros_like(local_tmax),
         ]
     )
-    every = voc_gather(stats, voc_count, 3)
+    (every,) = exchange([stats], [(voc_count,) + stats.shape], "voc", 9)
     teacher_max = jnp.max(every[:, 0], axis=0)
     student_max = jnp.max(every[:, 1], axis=0)
     teacher_scale = jnp.exp(every[:, 0] - teacher_max[None, :])

time: 382 us -> 361 us (0.945)
  Pallas kernels: 109 us -> 285 us
  waiting for transfers between devices: 96.4 us -> 4.2 us
  blocking collectives: 75.2 us -> 0 us
  local copies, waits for them, and re-layouts: 24.3 us -> 4.78 us
  matrix products: 36.2 us -> 28.1 us
  starting transfers between devices: 8.69 us -> 1.26 us
  other arithmetic: 17 us -> 23 us
    pallas_call x3 -> x7, Pallas kernels: 44.1 us -> 218 us  [the longest x6 162 us: exchange(): pl.pallas_call(functools.partial(exchange_kernel, axis, n, count, source,...]
    all_to_all x2 -> x0, blocking collectives: 75.2 us -> none  [the longest x1 52.5 us: per_device(): lax.all_to_all(outgoing, ('tok', 'voc'), split_axis=0, concat_axis=0, til...]
    reduce_scatter x1 -> x0, waiting for transfers between devices: 58.3 us -> none  [per_device(): lax.psum_scatter(teacher_part, 'tok', scatter_dimension=0, tiled=True)]
    all_to_all x1 -> x0, waiting for transfers between devices: 38 us -> none  [per_device(): lax.all_to_all(partial_out, ('tok', 'voc'), split_axis=0, concat_axis=0,...]
    reshape x4 -> x0, local copies, waits for them, and re-layouts: 13.8 us -> none  [the longest x1 4.42 us: per_device(): partial_out = jnp.dot(hidden_units, w_down, preferred_element_type=jnp.fl...]
    dot_general x3, matrix products: 13.7 us -> 5.06 us  [the longest x1 2.5 us: per_device(): lax.dot_general(matched.astype(jnp.bfloat16), tokens_all, (((0,), (0,)),...]
    all_to_all x1 -> x0, starting transfers between devices: 7.09 us -> none  [per_device(): lax.all_to_all(partial_out, ('tok', 'voc'), split_axis=0, concat_axis=0,...]
    broadcast_in_dim x1 -> x4, local copies, waits for them, and re-layouts: 5.08 us -> 0.77 us  [the longest x2 0.77 us: per_device(): jnp.broadcast_to(squares, (core_rows, 128)).reshape(chips, rows_here, 128)]
  transfers between devices with their start and end apart: 4 -> 4, of which waited for: 2 -> 1; matrix products, arithmetic and copies ran while one was open for 14% -> 12% of each run, Pallas kernels for 7% -> 60%
where the time goes in v3:
time: 361 us; the launch traced here: 360 us
  Pallas kernels  285 us (79%)
  matrix products  28.1 us (8%)
  other arithmetic  23 us (6%)
  between operations  14.3 us (4%)
  local copies, waits for them, and re-layouts  4.78 us (1%)
  waiting for transfers between devices  4.2 us (1%)
    pallas_call x6, Pallas kernels, exchange(): pl.pallas_call(functools.partial(exchange_kernel, axis, n, count, source,...  162 us
    pallas_call x1, Pallas kernels, grad_reduce(): pl.pallas_call(grad_kernel, out_shape=jax.ShapeDtypeStruct((rows // 2, wi...  67 us
    pallas_call x1, Pallas kernels, head_reduce(): pl.pallas_call(head_kernel, out_shape=jax.ShapeDtypeStruct((count, column...  55.3 us
    dot_general x1, matrix products, per_device(): jnp.dot(student_all, student_head, preferred_element_type=jnp.float32)  12.1 us
  transfers between devices with their start and end apart: 4, of which 1 were waited for; matrix products, arithmetic and copies ran while one was open for 12% of the time, Pallas kernels for 60%

profile of v3, /device:TPU:17, one launch (start us, length us, event | category | flops | bytes accessed | tf_op | source)
XLA Modules:
  0.0 360.1 jit_solution(3864815796580939484)
XLA Ops:
  7.2 0.7 all-gather.2.cloned.1.call-update
  8.0 0.8 convert_element_type.49
  8.9 1.4 maximum_maximum_fusion.refs_1_
  10.2 13.4 %shard_map.131 = (bf16[8,8,4096]{2,1,0:T(8,128)(2,1)}, f32[8,8,128]{2,1,0:T(8,128)}) custom-call(bf16[8,4096]{1,0:T(8,128)(2,1)} %refs_0_.1, f32[8,128]{1,0:T(8,128)} %maximum_maximum_fusion.refs_1_), custom_call_target="tpu_custom_call" | custom-call | tf_op jit(solution)/shard_map/pallas_call | solution.py:87
  23.6 1.2 fusion.61
  25.7 2.5 convolution_convert_fusion.1
  28.2 39.2 %shard_map.132 = bf16[16,16,4096]{2,1,0:T(8,128)(2,1)} custom-call(bf16[8,16,4096]{2,1,0:T(8,128)(2,1)} %bitcast.67), custom_call_target="tpu_custom_call" | custom-call | tf_op jit(solution)/shard_map/pallas_call | solution.py:87
  67.4 3.5 all-gather.2.cloned.1.call-done
  70.9 12.1 %fusion.62 = f32[1024,4864]{1,0:T(8,128)} fusion(bf16[1024,512]{1,0:T(8,128)(2,1)} %all-gather.2.cloned.1.call-done, bf16[512,4864]{1,0:T(8,128)(2,1)} %own_hbm.3), kind=kOutput, calls=%fused_computation.125 | convolution fusion | flops 5100273664 | bytes 25952256 | tf_op jit(solution)/shard_map/dot_general | solution.py:455
  83.1 0.9 collective-permute-start
  84.0 0.3 collective-permute-start.1
  84.5 4.5 %fusion.63 = f32[256,384]{1,0:T(8,128)} fusion(bf16[256,4096]{1,0:T(8,128)(2,1)} %bitcast.70, bf16[4096,384]{1,0:T(8,128)(2,1)} %param.15), kind=kOutput, calls=%fused_computation.126 | convolution fusion | flops 805306368 | bytes 5636096 | tf_op jit(solution)/shard_map/dot_general | solution.py:511
  89.1 6.3 %convolution_convert_fusion = bf16[256,4096]{1,0:T(8,128)(2,1)} fusion(bf16[384,4096]{1,0:T(8,128)(2,1)S(1)} %copy-done, bf16[256,4096]{1,0:T(8,128)(2,1)} %bitcast.71, bf16[4096,384]{1,0:T(8,128)(2,1)} %param.16, f32[256,384]{1,0:T(8,128)} %fusion.63), kind=kOutput, calls=%fused_computation | convolution fusion | flops 1612251136 | bytes 10878976 | tf_op jit(solution)/shard_map/dot_general | solution.py:514
  95.4 43.4 %shard_map.133 = bf16[16,16,4096]{2,1,0:T(8,128)(2,1)} custom-call(bf16[16,16,4096]{2,1,0:T(8,128)(2,1)} %bitcast.72), custom_call_target="tpu_custom_call" | custom-call | tf_op jit(solution)/shard_map/pallas_call | solution.py:87
  138.8 2.3 convert_reduce_fusion
  141.1 2.3 fusion.19.refs_0_
  143.4 25.7 %shard_map.134 = f32[8,32,1024]{2,1,0:T(8,128)} custom-call(f32[64,4096]{1,0:T(8,128)} %fusion.19.refs_0_), custom_call_target="tpu_custom_call" | custom-call | tf_op jit(solution)/shard_map/pallas_call | solution.py:87
  169.1 1.3 reduce_sum.128
  170.5 1.6 multiply_reduce_fusion.1
  172.2 0.7 broadcast_in_dim.133.refs_1_
  172.9 31.3 %shard_map.135 = (bf16[4,16,8,1024]{3,2,1,0:T(8,128)(2,1)}, f32[4,16,8,128]{3,2,1,0:T(8,128)}) custom-call(bf16[4,8,1024]{2,1,0:T(8,128)(2,1)} %get-tuple-element.30.refs_0_, f32[4,8,128]{2,1,0:T(8,128)} %broadcast_in_dim.133.refs_1_), custom_call_target="tpu_custom_call" | custom-call | tf_op jit(solution)/shard_map/pallas_call | solution.py:87
  204.2 55.3 %shard_map.136 = f32[128,4864]{1,0:T(8,128)} custom-call(bf16[4,128,1024]{2,1,0:T(8,128)(2,1)} %bitcast.73, f32[4,128,128]{2,1,0:T(8,128)} %bitcast.75, bf16[512,4864]{1,0:T(8,128)(2,1)} %own_hbm.2, bf16[512,4864]{1,0:T(8,128)(2,1)} %collective-permute-done.pair_hbm), custom_call_target="tpu_custom_call" | custom-call | tf_op jit(solution)/shard_map/pallas_call | solution.py:407
  259.5 2.0 reduce_max.36
  261.6 1.9 reduce_max.37
  263.5 5.0 %multiply_reduce_fusion = (f32[128]{0:T(128)S(1)}, f32[128]{0:T(128)S(1)}, f32[128]{0:T(128)S(1)}, f32[128,4864]{1,0:T(8,128)}, f32[128]{0:T(128)S(1)}, /*index=5*/f32[128]{0:T(128)S(1)}) fusion(f32[128,4864]{1,0:T(8,128)} %reduce-scatter.2.cloned.1.call-done, f32[128]{0:T(128)S(1)} %reduce_max.37, s32[128]{0:T(128)S(1)} %broadcast_subtract_fusion, ...), kind=kLoop, calls=%fused_computation.7 | loop fusion | flops 7470464 | bytes 7475200 | tf_op jit(solution)/shard_map/reduce_sum | solution.py:575
  268.5 0.6 stack.31.refs_0_
  269.1 9.2 %shard_map.137 = f32[16,8,128]{2,1,0:T(8,128)} custom-call(f32[8,128]{1,0:T(8,128)} %stack.31.refs_0_), custom_call_target="tpu_custom_call" | custom-call | tf_op jit(solution)/shard_map/pallas_call | solution.py:87
  278.3 1.2 fusion.60
  279.6 0.5 subtract_subtract_fusion
  280.2 4.6 %multiply_convert_fusion.g_ref = bf16[128,4864]{1,0:T(8,128)(2,1)} fusion(f32[128,4864]{1,0:T(8,128)} %get-tuple-element.26, f32[128,4864]{1,0:T(8,128)} %reduce-scatter.2.cloned.1.call-done, f32[128]{0:T(128)S(1)} %get-tuple-element.24, f32[128]{0:T(128)S(1)} %get-tuple-element.25, f32[128]{0:T(128)S(1)} %copy-done.4, s32[128]{0:T(128)S(1)} %broadcast_subtract_fusion), kind=kLoop, calls=%fused_computation.3 | loop fusion | flops 5603328 | bytes 6227968 | tf_op jit(solution)/shard_map/convert_element_type | solution.py:601
  284.8 67.0 %shard_map.138 = bf16[64,512]{1,0:T(8,128)(2,1)} custom-call(bf16[128,4864]{1,0:T(8,128)(2,1)} %multiply_convert_fusion.g_ref, bf16[512,4864]{1,0:T(8,128)(2,1)} %own_hbm.3, bf16[512,4864]{1,0:T(8,128)(2,1)} %collective-permute-done.1.pair_hbm), custom_call_target="tpu_custom_call" | custom-call | tf_op jit(solution)/shard_map/pallas_call | solution.py:241
  351.8 1.5 copy.43
  (45 shorter events, 1.5 us)
Async XLA Ops:
  7.2 81.9 %copy-start = (bf16[384,4096]{1,0:T(8,128)(2,1)S(1)}, bf16[384,4096]{1,0:T(8,128)(2,1)}, u32[]{:S(2)}) copy-start(bf16[384,4096]{1,0:T(8,128)(2,1)} %param.17) | copy-start | bytes 9437188
  7.2 63.7 %all-gather.2.cloned.1.call-start = ((), (), s32[]{:S(2)}) async-start(), calls=%async_computation.1 | async-start | bytes 1114112 | tf_op jit(solution)/shard_map/all_gather | solution.py:454
  7.9 253.7 %reduce-scatter.2.cloned.1.call-start = ((), (), s32[]{:S(2)}) async-start(), calls=%async_computation.2 | async-start | bytes 22413312 | tf_op jit(solution)/shard_map/reduce_scatter | solution.py:509
  83.0 1.2 copy-start.3
  83.0 1.4 copy-start.5
  83.1 121.1 %collective-permute-start = (bf16[512,4864]{1,0:T(8,128)(2,1)}, bf16[512,4864]{1,0:T(8,128)(2,1)}, u32[]{:S(2)}, u32[]{:S(2)}) collective-permute-start(bf16[512,4864]{1,0:T(8,128)(2,1)} %own_hbm.2), channel_id=1, source_target_pairs={{0,16},{16,0},{32,48},{48,32},{64,80},{80,64},{96,112},{112,96},{1... | collective-permute-start | bytes 14942216 | tf_op jit(solution)/shard_map/ppermute | solution.py:453
  84.0 200.8 %collective-permute-start.1 = (bf16[512,4864]{1,0:T(8,128)(2,1)}, bf16[512,4864]{1,0:T(8,128)(2,1)}, u32[]{:S(2)}, u32[]{:S(2)}) collective-permute-start(bf16[512,4864]{1,0:T(8,128)(2,1)} %own_hbm.3), channel_id=1, source_target_pairs={{0,16},{16,0},{32,48},{48,32},{64,80},{80,64},{96,112},{112,96},{1... | collective-permute-start | bytes 14942216 | tf_op jit(solution)/shard_map/ppermute | solution.py:452
  141.1 29.4 %dynamic-slice-start = ((f32[4096]{0:T(1024)}, s32[]{:T(128)}), f32[1024]{0:T(1024)S(1)}, s32[]{:S(2)}) async-start(f32[4096]{0:T(1024)} %param.18, s32[]{:T(128)} %select_n.112), calls=%async_computation.3 | async-start | bytes 8704 | tf_op jit(solution)/shard_map/dynamic_slice | solution.py:539
  259.5 4.0 %copy-start.2 = (f32[128,4864]{1,0:T(8,128)S(1)}, f32[128,4864]{1,0:T(8,128)}, u32[]{:S(2)}) copy-start(f32[128,4864]{1,0:T(8,128)} %shard_map.136) | copy-start | bytes 7471108
  263.5 16.7 %copy-start.4 = (f32[128]{0:T(128)S(1)}, f32[128]{0:T(128)}, u32[]{:S(2)}) copy-start(f32[128]{0:T(128)} %param.23) | copy-start | bytes 1540
  284.8 68.5 %copy-start.1 = (bf16[384,4096]{1,0:T(8,128)(2,1)S(1)}, bf16[384,4096]{1,0:T(8,128)(2,1)}, u32[]{:S(2)}) copy-start(bf16[384,4096]{1,0:T(8,128)(2,1)} %param.17) | copy-start | bytes 9437188
Sparse Core Ops, SparseCore 0:
  10.1 60.7 all-gather.1
  83.2 122.8 reduce-scatter.1

commit v4 on v3

--- a/solution.py
+++ b/solution.py
@@ -9,51 +9,56 @@
 MESH = pl.DeviceIdType.MESH
 
 
-def exchange_kernel(axis, n, count, source, target, *refs):
+def device_on(axis, index):
+    if axis == "tok":
+        return (index, lax.axis_index("voc"))
+    return (lax.axis_index("tok"), index)
+
+
+def exchange_kernel(axes, sizes, source, targets, *refs):
+    count = len(axes)
     ins, outs = refs[:count], refs[count : 2 * count]
     send_sem, recv_sem, own_sem = refs[2 * count :]
-    me = lax.axis_index(axis)
-
-    def device(k):
+    barrier = pltpu.get_barrier_semaphore()
+    for axis in sorted(set(axes)):
+        n = sizes[axis]
+
+        @pl.loop(1, n)
+        def _(k):
+            peer = lax.rem(lax.axis_index(axis) + k, n)
+            pl.semaphore_signal(barrier, inc=1, device_id=device_on(axis, peer), device_id_type=MESH)
+
+    pl.semaphore_wait(barrier, sum(sizes[axis] - 1 for axis in set(axes)))
+
+    def copy(i, k, back):
+        me, n = lax.axis_index(axes[i]), sizes[axes[i]]
         peer = lax.rem(me + k, n)
-        if axis == "tok":
-            return (peer, lax.axis_index("voc"))
-        return (lax.axis_index("tok"), peer)
-
-    barrier = pltpu.get_barrier_semaphore()
-
-    @pl.loop(1, n)
-    def _(k):
-        pl.semaphore_signal(barrier, inc=1, device_id=device(k), device_id_type=MESH)
-
-    pl.semaphore_wait(barrier, n - 1)
-
-    def copy(i, k, sender):
         return pltpu.make_async_remote_copy(
-            src_ref=source(ins[i], lax.rem(me + k, n)),
-            dst_ref=target(outs[i], sender),
+            src_ref=source(ins[i], peer),
+            dst_ref=targets[i](outs[i], lax.rem(me - k + n, n) if back else me),
             send_sem=send_sem.at[i, k],
             recv_sem=recv_sem.at[i, k],
-            device_id=device(k),
+            device_id=device_on(axes[i], peer),
             device_id_type=MESH,
         )
 
     for i in range(count):
 
-        @pl.loop(1, n)
+        @pl.loop(1, sizes[axes[i]])
         def _(k):
-            copy(i, k, me).start()
+            copy(i, k, False).start()
 
     for i in range(count):
-        own = pltpu.make_async_copy(source(ins[i], me), target(outs[i], me), own_sem)
+        me = lax.axis_index(axes[i])
+        own = pltpu.make_async_copy(source(ins[i], me), targets[i](outs[i], me), own_sem)
         own.start()
         own.wait()
 
     for i in range(count):
 
-        @pl.loop(1, n)
+        @pl.loop(1, sizes[axes[i]])
         def _(k):
-            copy(i, k, lax.rem(me - k + n, n)).wait()
+            copy(i, k, True).wait()
 
 
 def whole(ref, peer):
@@ -81,21 +86,142 @@
     return ref.at[rows, pl.ds(pl.multiple_of((peer // 2) * 1024, 1024), 1024)]
 
 
-def exchange(arrays, shapes, axis, collective_id, source=whole, target=at_peer):
-    n = lax.axis_size(axis)
+def exchange(arrays, shapes, axes, collective_id, source=whole, targets=None):
     count = len(arrays)
+    sizes = {axis: lax.axis_size(axis) for axis in axes}
     return pl.pallas_call(
-        functools.partial(exchange_kernel, axis, n, count, source, target),
+        functools.partial(
+            exchange_kernel, axes, sizes, source, targets or (at_peer,) * count
+        ),
         out_shape=[jax.ShapeDtypeStruct(o, x.dtype) for o, x in zip(shapes, arrays)],
         in_specs=[pl.BlockSpec(memory_space=pltpu.VMEM)] * count,
         out_specs=[pl.BlockSpec(memory_space=pltpu.VMEM)] * count,
         scratch_shapes=[
-            pltpu.SemaphoreType.DMA((count, n)),
-            pltpu.SemaphoreType.DMA((count, n)),
+            pltpu.SemaphoreType.DMA((count, max(sizes.values()))),
+            pltpu.SemaphoreType.DMA((count, max(sizes.values()))),
             pltpu.SemaphoreType.DMA,
         ],
         compiler_params=pltpu.CompilerParams(collective_id=collective_id, has_side_effects=True),
     )(*arrays)
+
+
+OFFSETS = (
+    (0, 1), (1, 0), (0, 3), (3, 0), (1, 1), (3, 3), (1, 3),
+    (3, 1), (2, 0), (0, 2), (1, 2), (2, 1), (3, 2), (2, 3), (2, 2),
+)
+
+
+def expert_kernel(
+    x_ref, gate_hbm, up_hbm, down_hbm, out_ref,
+    gate_w, up_w, down_w, rows, results,
+    load_sem, rows_send, rows_recv, back_send, back_recv, own_sem,
+):
+    v = lax.axis_index("voc")
+    y, z = v // 4, lax.rem(v, 4)
+    loads = [
+        pltpu.make_async_copy(source, target, load_sem.at[i])
+        for i, (source, target) in enumerate(
+            ((gate_hbm, gate_w), (up_hbm, up_w), (down_hbm, down_w))
+        )
+    ]
+    for load in loads:
+        load.start()
+
+    def ahead(i):
+        dy, dz = OFFSETS[i - 1]
+        return lax.rem(y + dy, 4) * 4 + lax.rem(z + dz, 4)
+
+    def behind(i):
+        dy, dz = OFFSETS[i - 1]
+        return lax.rem(y + 4 - dy, 4) * 4 + lax.rem(z + 4 - dz, 4)
+
+    barrier = pltpu.get_barrier_semaphore()
+    for i in range(1, 16):
+        pl.semaphore_signal(
+            barrier, inc=1, device_id=device_on("voc", ahead(i)), device_id_type=MESH
+        )
+    pl.semaphore_wait(barrier, 15)
+
+    def row_copy(i):
+        return pltpu.make_async_remote_copy(
+            src_ref=x_ref.at[ahead(i) // 2],
+            dst_ref=rows.at[i],
+            send_sem=rows_send.at[i],
+            recv_sem=rows_recv.at[i],
+            device_id=device_on("voc", ahead(i)),
+            device_id_type=MESH,
+        )
+
+    def back_copy(i, place):
+        return pltpu.make_async_remote_copy(
+            src_ref=results.at[i],
+            dst_ref=out_ref.at[place],
+            send_sem=back_send.at[i],
+            recv_sem=back_recv.at[i],
+            device_id=device_on("voc", behind(i)),
+            device_id_type=MESH,
+        )
+
+    for i in range(1, 16):
+        row_copy(i).start()
+    own = pltpu.make_async_copy(x_ref.at[v // 2], rows.at[0], own_sem.at[0])
+    own.start()
+    for load in loads:
+        load.wait()
+    own.wait()
+    group, width = rows.shape[1:]
+    step = 512
+    own_back = pltpu.make_async_copy(results.at[0], out_ref.at[v], own_sem.at[1])
+    for first in (0, 8):
+        for i in range(max(first, 1), first + 8):
+            row_copy(i).wait_recv()
+        batch = rows[pl.ds(first, 8)].reshape(8 * group, width)
+        gate = jnp.dot(batch, gate_w[...], preferred_element_type=jnp.float32)
+        up = jnp.dot(batch, up_w[...], preferred_element_type=jnp.float32)
+        units = (gate * jax.nn.sigmoid(gate) * up).astype(jnp.bfloat16)
+
+        @pl.loop(0, width // step)
+        def _(j):
+            columns = pl.ds(pl.multiple_of(j * step, step), step)
+            part = jnp.dot(units, down_w[:, columns], preferred_element_type=jnp.float32)
+            results[pl.ds(first, 8), :, columns] = part.astype(jnp.bfloat16).reshape(8, group, step)
+
+        for i in range(max(first, 1), first + 8):
+            back_copy(i, v).start()
+        if first == 0:
+            own_back.start()
+    own_back.wait()
+    for i in range(1, 16):
+        row_copy(i).wait_send()
+        back_copy(i, ahead(i)).wait()
+
+
+def expert_layer(x, w_gate, w_up, w_down, collective_id):
+    _, group, width = x.shape
+    vmem = pl.BlockSpec(memory_space=pltpu.VMEM)
+    hbm = pl.BlockSpec(memory_space=pl.ANY)
+    return pl.pallas_call(
+        expert_kernel,
+        out_shape=jax.ShapeDtypeStruct((16, group, width), jnp.bfloat16),
+        in_specs=[vmem, hbm, hbm, hbm],
+        out_specs=vmem,
+        scratch_shapes=[
+            pltpu.VMEM(w_gate.shape, jnp.bfloat16),
+            pltpu.VMEM(w_up.shape, jnp.bfloat16),
+            pltpu.VMEM(w_down.shape, jnp.bfloat16),
+            pltpu.VMEM((16, group, width), jnp.bfloat16),
+            pltpu.VMEM((16, group, width), jnp.bfloat16),
+            pltpu.SemaphoreType.DMA((3,)),
+            pltpu.SemaphoreType.DMA((16,)),
+            pltpu.SemaphoreType.DMA((16,)),
+            pltpu.SemaphoreType.DMA((16,)),
+            pltpu.SemaphoreType.DMA((16,)),
+            pltpu.SemaphoreType.DMA((2,)),
+        ],
+        compiler_params=pltpu.CompilerParams(
+            collective_id=collective_id, has_side_effects=True, vmem_limit_bytes=56 * 1024 * 1024
+        ),
+    )(x, w_gate, w_up, w_down)
 
 
 def grad_kernel(
@@ -451,19 +577,24 @@
     part_width = model_width // tok_count
     student_pair = lax.ppermute(student_head, "tok", [(i, i ^ 1) for i in range(tok_count)])
     teacher_pair = lax.ppermute(teacher_head, "tok", [(i, i ^ 1) for i in range(tok_count)])
-    student_all = lax.all_gather(student_hidden, "voc", axis=0, tiled=True)
-    student_part = jnp.dot(student_all, student_head, preferred_element_type=jnp.float32)
     ids_shares = jnp.concatenate(
         [expert_ids.astype(jnp.float32), gate_raw, jnp.zeros((rows_here, 128 - 2 * top_k), jnp.float32)],
         axis=1,
     )
     rows_all = tok_count * rows_here
-    tokens_all, table = exchange(
-        [tokens_in, ids_shares],
-        [(tok_count, rows_here, model_width), (tok_count, rows_here, 128)],
-        "tok",
+    student_all, tokens_all, table = exchange(
+        [student_hidden, tokens_in, ids_shares],
+        [
+            (voc_count,) + student_hidden.shape,
+            (tok_count, rows_here, model_width),
+            (tok_count, rows_here, 128),
+        ],
+        ("voc", "tok", "tok"),
         2,
-        target=at_core_chip,
+        targets=(at_peer, at_core_chip, at_core_chip),
+    )
+    student_part = jnp.dot(
+        student_all.reshape(-1, part_width), student_head, preferred_element_type=jnp.float32
     )
     tokens_all = tokens_all.reshape(rows_all, model_width)
     table = table.reshape(rows_all, 128)
@@ -498,28 +629,10 @@
         preferred_element_type=jnp.float32,
     ).astype(jnp.bfloat16)
     group = tok_count * slots
-    (arrived,) = exchange(
-        [dispatched.reshape(here, group, model_width)],
-        [(voc_count, group, model_width)],
-        "voc",
-        3,
-        source=at_pair,
-    )
-    arrived, student_part = lax.optimization_barrier((arrived, student_part))
+    dispatched, student_part = lax.optimization_barrier((dispatched, student_part))
     student_logits = lax.psum_scatter(student_part, "tok", scatter_dimension=0, tiled=True)
-    expert_rows = arrived.reshape(voc_count * group, model_width)
-    gate_part = jnp.dot(expert_rows, w_gate, preferred_element_type=jnp.float32)
-    up_part = jnp.dot(expert_rows, w_up, preferred_element_type=jnp.float32)
-    hidden_units = (jax.nn.silu(gate_part) * up_part).astype(jnp.bfloat16)
-    partial_out = jnp.dot(hidden_units, w_down, preferred_element_type=jnp.float32).astype(
-        jnp.bfloat16
-    )
-    (returned,) = exchange(
-        [partial_out.reshape(voc_count, group, model_width)],
-        [(voc_count, group, model_width)],
-        "voc",
-        5,
-        source=at_peer,
+    returned = expert_layer(
+        dispatched.reshape(here, group, model_width), w_gate, w_up, w_down, 3
     )
     pair_sum = jnp.sum(
         returned.astype(jnp.float32).reshape(here, 2, group, model_width), axis=1
@@ -527,14 +640,18 @@
     mix_part = jnp.dot(combine_table, pair_sum, precision=lax.Precision.HIGHEST)
     core_rows, chip_width = rows_all // 2, 2 * part_width
     (mix_parts,) = exchange(
-        [mix_part], [(tok_count, core_rows, chip_width)], "tok", 6, source=at_core_features
+        [mix_part.astype(jnp.bfloat16)],
+        [(tok_count, core_rows, chip_width)],
+        ("tok",),
+        6,
+        source=at_core_features,
     )
     tok_index = lax.axis_index("tok")
     feature_start = (tok_index // 2) * chip_width
     tokens_part = lax.dynamic_slice(
         tokens_all, ((tok_index % 2) * core_rows, feature_start), (core_rows, chip_width)
     )
-    residual_sum = tokens_part.astype(jnp.float32) + jnp.sum(mix_parts, axis=0)
+    residual_sum = tokens_part.astype(jnp.float32) + jnp.sum(mix_parts.astype(jnp.float32), axis=0)
     squares = jnp.sum(residual_sum * residual_sum, axis=1, keepdims=True)
     gain_part = lax.dynamic_slice_in_dim(final_gain, feature_start, chip_width, 0)
     scaled = (residual_sum * gain_part[None, :]).astype(jnp.bfloat16)
@@ -548,9 +665,9 @@
             (chips, voc_count, rows_here, chip_width),
             (chips, voc_count, rows_here, 128),
         ],
-        "voc",
+        ("voc", "voc"),
         8,
-        target=at_second,
+        targets=(at_second, at_second),
     )
     vocab_local = teacher_head.shape[1]
     teacher_logits = head_reduce(
@@ -578,7 +695,7 @@
             jnp.zeros_like(local_tmax),
         ]
     )
-    (every,) = exchange([stats], [(voc_count,) + stats.shape], "voc", 9)
+    (every,) = exchange([stats], [(voc_count,) + stats.shape], ("voc",), 9)
     teacher_max = jnp.max(every[:, 0], axis=0)
     student_max = jnp.max(every[:, 1], axis=0)
     teacher_scale = jnp.exp(every[:, 0] - teacher_max[None, :])

time: 361 us -> 316 us (0.88)
  Pallas kernels: 285 us -> 253 us
  matrix products: 28.1 us -> 16.9 us
  waiting for transfers between devices: 4.2 us -> 0.04 us
    pallas_call x6 -> x5, Pallas kernels: 162 us -> 132 us  [the longest x4 74.3 us: exchange(): pl.pallas_call(functools.partial(exchange_kernel, axes, sizes, source, ta...]
    dot_general x3 -> x1, matrix products: 23 us -> 11.9 us  [per_device(): jnp.dot(student_all.reshape(-1, part_width), student_head, preferred_elem...]
  transfers between devices with their start and end apart: 4 -> 3, of which waited for: 1 -> 0; matrix products, arithmetic and copies ran while one was open for 12% -> 8% of each run, Pallas kernels for 60% -> 53%
where the time goes in v4:
time: 316 us; the launch traced here: 315 us
  Pallas kernels  253 us (80%)
  other arithmetic  22.9 us (7%)
  matrix products  16.9 us (5%)
  between operations  14.3 us (5%)
  local copies, waits for them, and re-layouts  5.61 us (2%)
    pallas_call x4, Pallas kernels, exchange(): pl.pallas_call(functools.partial(exchange_kernel, axes, sizes, source, ta...  74.3 us
    pallas_call x1, Pallas kernels, grad_reduce(): pl.pallas_call(grad_kernel, out_shape=jax.ShapeDtypeStruct((rows // 2, wi...  63.7 us
    pallas_call x1, Pallas kernels, head_reduce(): pl.pallas_call(head_kernel, out_shape=jax.ShapeDtypeStruct((count, column...  57.8 us
    pallas_call x1, Pallas kernels, expert_layer(): pl.pallas_call(expert_kernel, out_shape=jax.ShapeDtypeStruct((16, group,...  57.7 us
    dot_general x1, matrix products, per_device(): jnp.dot(student_all.reshape(-1, part_width), student_head, preferred_elem...  11.9 us
  transfers between devices with their start and end apart: 3, of which 0 were waited for; matrix products, arithmetic and copies ran while one was open for 8% of the time, Pallas kernels for 53%

profile of v4, /device:TPU:17, one launch (start us, length us, event | category | flops | bytes accessed | tf_op | source)
XLA Modules:
  0.0 315.1 jit_solution(7323728619075098591)
XLA Ops:
  7.2 0.7 convert_element_type.49
  7.9 0.1 pad.2.clone
  8.0 1.4 maximum_maximum_fusion.refs_2_
  9.4 22.1 %shard_map.131 = (bf16[16,64,512]{2,1,0:T(8,128)(2,1)}, bf16[8,8,4096]{2,1,0:T(8,128)(2,1)}, f32[8,8,128]{2,1,0:T(8,128)}) custom-call(bf16[64,512]{1,0:T(8,128)(2,1)} %refs_0_.1, bf16[8,4096]{1,0:T(8,128)(2,1)} %refs_1_.1, f32[8,128]{1,0:T(8,128)} %maximum_maximum_fusion.refs_2_), custom_call_target="tpu_custom_call" | custom-call | tf_op jit(solution)/shard_map/pallas_call | solution.py:92
  31.5 1.3 fusion.52
  33.4 0.3 fusion.2
  33.7 2.5 convolution_convert_fusion
  36.2 11.9 %fusion.53 = f32[1024,4864]{1,0:T(8,128)} fusion(bf16[1024,512]{1,0:T(8,128)(2,1)S(1)} %bitcast.97, bf16[512,4864]{1,0:T(8,128)(2,1)} %own_hbm.3), kind=kOutput, calls=%fused_computation.116 | convolution fusion | flops 5100273664 | bytes 25952256 | tf_op jit(solution)/shard_map/dot_general | solution.py:596
  48.2 1.6 collective-permute-start
  49.8 0.3 collective-permute-start.1
  50.1 0.2 slice_reduce_fusion.2
  50.3 57.7 %shard_map.132 = bf16[16,16,4096]{2,1,0:T(8,128)(2,1)} custom-call(bf16[8,16,4096]{2,1,0:T(8,128)(2,1)} %bitcast.61, bf16[4096,384]{1,0:T(8,128)(2,1)} %gate_hbm.1, bf16[4096,384]{1,0:T(8,128)(2,1)} %up_hbm.1, bf16[384,4096]{1,0:T(8,128)(2,1)} %down_hbm.1), custom_call_target="tpu_custom_call" | custom-call | tf_op jit(solution)/shard_map/pallas_call | solution.py:203
  108.0 2.5 convert_reduce_fusion
  110.6 2.1 convolution_convert_fusion.1.refs_0_
  112.7 16.8 %shard_map.133 = bf16[8,32,1024]{2,1,0:T(8,128)(2,1)} custom-call(bf16[64,4096]{1,0:T(8,128)(2,1)} %convolution_convert_fusion.1.refs_0_), custom_call_target="tpu_custom_call" | custom-call | tf_op jit(solution)/shard_map/pallas_call | solution.py:92
  129.5 0.7 dynamic_slice.7
  130.2 1.1 convert_reduce_fusion.1
  131.4 1.6 multiply_reduce_fusion.1
  133.0 0.1 broadcast_in_dim.132
  133.1 0.7 broadcast_in_dim.133.refs_1_
  133.7 26.7 %shard_map.134 = (bf16[4,16,8,1024]{3,2,1,0:T(8,128)(2,1)}, f32[4,16,8,128]{3,2,1,0:T(8,128)}) custom-call(bf16[4,8,1024]{2,1,0:T(8,128)(2,1)} %get-tuple-element.32.refs_0_, f32[4,8,128]{2,1,0:T(8,128)} %broadcast_in_dim.133.refs_1_), custom_call_target="tpu_custom_call" | custom-call | tf_op jit(solution)/shard_map/pallas_call | solution.py:92
  160.5 57.8 %shard_map.135 = f32[128,4864]{1,0:T(8,128)} custom-call(bf16[4,128,1024]{2,1,0:T(8,128)(2,1)} %bitcast.64, f32[4,128,128]{2,1,0:T(8,128)} %bitcast.66, bf16[512,4864]{1,0:T(8,128)(2,1)} %own_hbm.2, bf16[512,4864]{1,0:T(8,128)(2,1)} %collective-permute-done.pair_hbm), custom_call_target="tpu_custom_call" | custom-call | tf_op jit(solution)/shard_map/pallas_call | solution.py:533
  218.4 2.0 reduce_max.36
  220.4 1.9 reduce_max.37
  222.3 5.0 %multiply_reduce_fusion = (f32[128]{0:T(128)S(1)}, f32[128]{0:T(128)S(1)}, f32[128]{0:T(128)S(1)}, f32[128,4864]{1,0:T(8,128)}, f32[128]{0:T(128)S(1)}, /*index=5*/f32[128]{0:T(128)S(1)}) fusion(f32[128,4864]{1,0:T(8,128)} %reduce-scatter.2.cloned.1.call-done, f32[128]{0:T(128)S(1)} %reduce_max.37, s32[128]{0:T(128)S(1)} %broadcast_subtract_fusion, ...), kind=kLoop, calls=%fused_computation.7 | loop fusion | flops 7470464 | bytes 7475200 | tf_op jit(solution)/shard_map/reduce_sum | solution.py:692
  227.3 0.6 stack.31.refs_0_
  227.9 8.7 %shard_map.136 = f32[16,8,128]{2,1,0:T(8,128)} custom-call(f32[8,128]{1,0:T(8,128)} %stack.31.refs_0_), custom_call_target="tpu_custom_call" | custom-call | tf_op jit(solution)/shard_map/pallas_call | solution.py:92
  236.6 1.2 fusion.51
  237.9 0.5 subtract_subtract_fusion
  238.5 4.6 %multiply_convert_fusion.g_ref = bf16[128,4864]{1,0:T(8,128)(2,1)} fusion(f32[128,4864]{1,0:T(8,128)} %get-tuple-element.28, f32[128,4864]{1,0:T(8,128)} %reduce-scatter.2.cloned.1.call-done, f32[128]{0:T(128)S(1)} %get-tuple-element.26, f32[128]{0:T(128)S(1)} %get-tuple-element.27, f32[128]{0:T(128)S(1)} %copy-done.2, s32[128]{0:T(128)S(1)} %broadcast_subtract_fusion), kind=kLoop, calls=%fused_computation.3 | loop fusion | flops 5603328 | bytes 6227968 | tf_op jit(solution)/shard_map/convert_element_type | solution.py:718
  243.1 63.7 %shard_map.137 = bf16[64,512]{1,0:T(8,128)(2,1)} custom-call(bf16[128,4864]{1,0:T(8,128)(2,1)} %multiply_convert_fusion.g_ref, bf16[512,4864]{1,0:T(8,128)(2,1)} %own_hbm.3, bf16[512,4864]{1,0:T(8,128)(2,1)} %collective-permute-done.1.pair_hbm), custom_call_target="tpu_custom_call" | custom-call | tf_op jit(solution)/shard_map/pallas_call | solution.py:367
  306.8 1.5 copy.43
  (36 shorter events, 0.8 us)
Async XLA Ops:
  7.2 213.3 %reduce-scatter.2.cloned.1.call-start = ((), (), s32[]{:S(2)}) async-start(), calls=%async_computation.1 | async-start | bytes 22413312 | tf_op jit(solution)/shard_map/reduce_scatter | solution.py:633
  31.5 4.8 %copy-start.3 = (bf16[16,64,512]{2,1,0:T(8,128)(2,1)S(1)}, bf16[16,64,512]{2,1,0:T(8,128)(2,1)}, u32[]{:S(2)}) copy-start(bf16[16,64,512]{2,1,0:T(8,128)(2,1)} %get-tuple-element.11) | copy-start | bytes 3145732
  48.2 1.9 copy-start.1
  48.2 112.3 %collective-permute-start = (bf16[512,4864]{1,0:T(8,128)(2,1)}, bf16[512,4864]{1,0:T(8,128)(2,1)}, u32[]{:S(2)}, u32[]{:S(2)}) collective-permute-start(bf16[512,4864]{1,0:T(8,128)(2,1)} %own_hbm.2), channel_id=1, source_target_pairs={{0,16},{16,0},{32,48},{48,32},{64,80},{80,64},{96,112},{112,96},{1... | collective-permute-start | bytes 14942216 | tf_op jit(solution)/shard_map/ppermute | solution.py:579
  49.8 193.3 %collective-permute-start.1 = (bf16[512,4864]{1,0:T(8,128)(2,1)}, bf16[512,4864]{1,0:T(8,128)(2,1)}, u32[]{:S(2)}, u32[]{:S(2)}) collective-permute-start(bf16[512,4864]{1,0:T(8,128)(2,1)} %own_hbm.3), channel_id=1, source_target_pairs={{0,16},{16,0},{32,48},{48,32},{64,80},{80,64},{96,112},{112,96},{1... | collective-permute-start | bytes 14942216 | tf_op jit(solution)/shard_map/ppermute | solution.py:578
  110.5 50.0 %copy-start.4 = (s32[128]{0:T(128)S(1)}, s32[128]{0:T(128)}, u32[]{:S(2)}) copy-start(s32[128]{0:T(128)} %param.22) | copy-start | bytes 1540
  218.4 4.0 %copy-start = (f32[128,4864]{1,0:T(8,128)S(1)}, f32[128,4864]{1,0:T(8,128)}, u32[]{:S(2)}) copy-start(f32[128,4864]{1,0:T(8,128)} %shard_map.135) | copy-start | bytes 7471108
  222.3 16.1 %copy-start.2 = (f32[128]{0:T(128)S(1)}, f32[128]{0:T(128)}, u32[]{:S(2)}) copy-start(f32[128]{0:T(128)} %param.23) | copy-start | bytes 1540
Sparse Core Ops, SparseCore 0:
  48.3 114.5 reduce-scatter.1

commit v5 on v4

--- a/solution.py
+++ b/solution.py
@@ -224,51 +224,267 @@
     )(x, w_gate, w_up, w_down)
 
 
-def grad_kernel(
-    g_ref, own_hbm, pair_hbm, out_ref,
-    own_w, pair_w, blocks, terms, landed,
-    load_sem, ring_send, ring_recv, term_send, term_recv, self_sem,
+def loss_kernel(
+    rows_ref, squares_ref, ids_ref, weight_ref,
+    head_own_hbm, head_pair_hbm, own_hbm, pair_hbm, student_hbm,
+    loss_ref, out_ref,
+    head_own, head_pair, own_w, pair_w, student,
+    far, kept, relay, sent, final, squares, logits,
+    columns_stat, stat, stats, grads, blocks, terms, landed,
+    load_sem, head_send, head_recv, square_send, square_recv, stat_send, stat_recv,
+    ring_send, ring_recv, term_send, term_recv, self_sem,
 ):
     t, v = lax.axis_index("tok"), lax.axis_index("voc")
     core = lax.rem(t, 2)
     chip = t // 2
     partner = t + 1 - 2 * core
-    right, left = lax.rem(t + 2, 8), lax.rem(t + 6, 8)
-    half = g_ref.shape[0] // 2
+    right, left, across = lax.rem(t + 2, 8), lax.rem(t + 6, 8), lax.rem(t + 4, 8)
+    count, vocab = grads.shape
+    half = count // 2
     source_core = lax.rem(v // 2, 2)
-    loads = (
-        pltpu.make_async_copy(own_hbm, own_w, load_sem.at[0]),
-        pltpu.make_async_copy(pair_hbm, pair_w, load_sem.at[1]),
-    )
-    for load in loads:
+    width = own_w.shape[0]
+    features = rows_ref.shape[2] * 4
+    step = 256
+    steps = vocab // step
+    top, low = pl.ds(0, half), pl.ds(half, half)
+    loads = [
+        pltpu.make_async_copy(source, target, load_sem.at[i])
+        for i, (source, target) in enumerate(
+            (
+                (head_own_hbm, head_own),
+                (head_pair_hbm, head_pair),
+                (student_hbm, student),
+                (own_hbm, own_w),
+                (pair_hbm, pair_w),
+            )
+        )
+    ]
+    for load in loads[:2]:
         load.start()
-
     barrier = pltpu.get_barrier_semaphore()
-    for side in (right, left):
+    for side in (right, left, across):
         pl.semaphore_signal(barrier, inc=1, device_id=(side, v), device_id_type=MESH)
 
     @pl.loop(0, 16)
     def _(k):
-        @pl.when(jnp.logical_or(source_core != core, k != v))
-        def _():
-            pl.semaphore_signal(
-                barrier, inc=1, device_id=(chip * 2 + source_core, k), device_id_type=MESH
+        pl.semaphore_signal(barrier, inc=1, device_id=(partner, k), device_id_type=MESH)
+
+    @pl.loop(1, 16)
+    def _(k):
+        pl.semaphore_signal(
+            barrier, inc=1, device_id=(t, lax.rem(v + k, 16)), device_id_type=MESH
+        )
+
+    pl.semaphore_wait(barrier, 34)
+
+    chips = [lax.rem(chip + shift, 4) for shift in range(4)]
+    square_copies = [
+        pltpu.make_async_remote_copy(
+            src_ref=squares_ref.at[chips[shift]],
+            dst_ref=squares.at[shift - 1],
+            send_sem=square_send.at[shift - 1],
+            recv_sem=square_recv.at[shift - 1],
+            device_id=(device, v),
+            device_id_type=MESH,
+        )
+        for shift, device in ((1, right), (2, across), (3, left))
+    ]
+    head_plan = (
+        (far.at[top], relay.at[0], right),
+        (far.at[low], relay.at[1], left),
+        (sent.at[0, low], final.at[0, low], right),
+        (sent.at[1, top], final.at[1, top], left),
+        (sent.at[0, top], final.at[0, top], right),
+        (sent.at[1, low], final.at[1, low], left),
+    )
+    head_ring = [
+        pltpu.make_async_remote_copy(
+            src_ref=source,
+            dst_ref=target,
+            send_sem=head_send.at[i],
+            recv_sem=head_recv.at[i],
+            device_id=(device, v),
+            device_id_type=MESH,
+        )
+        for i, (source, target, device) in enumerate(head_plan)
+    ]
+    own_columns = pl.ds(pl.multiple_of(core * width, width), width)
+    pair_columns = pl.ds(pl.multiple_of((1 - core) * width, width), width)
+
+    def head_part(shift, store):
+        own_rows = rows_ref[chips[shift], :, own_columns]
+        pair_rows = rows_ref[chips[shift], :, pair_columns]
+
+        @pl.loop(0, steps)
+        def _(j):
+            columns = pl.ds(pl.multiple_of(j * step, step), step)
+            store(
+                columns,
+                jnp.dot(own_rows, head_own[:, columns], preferred_element_type=jnp.float32)
+                + jnp.dot(pair_rows, head_pair[:, columns], preferred_element_type=jnp.float32),
             )
 
-    @pl.when(source_core == core)
-    def _():
-        pl.semaphore_wait(barrier, 17)
-
-    @pl.when(source_core != core)
-    def _():
-        pl.semaphore_wait(barrier, 18)
-
-    top, low = pl.ds(0, half), pl.ds(half, half)
+    def store_far(columns, value):
+        far[:, columns] = value.astype(jnp.bfloat16)
+
+    def store_right(columns, value):
+        kept[0, :, columns] = value[:half]
+        sent[0, low, columns] = value[half:].astype(jnp.bfloat16)
+
+    def store_left(columns, value):
+        kept[1, :, columns] = value[half:]
+        sent[1, top, columns] = value[:half].astype(jnp.bfloat16)
+
+    def store_own(columns, value):
+        logits[:, columns] = value
+
+    for load in loads[:2]:
+        load.wait()
+    for load in loads[2:]:
+        load.start()
+    head_part(2, store_far)
+    head_ring[0].start()
+    head_ring[1].start()
+    head_part(1, store_right)
+    head_ring[2].start()
+    head_part(3, store_left)
+    head_ring[3].start()
+    for copy in square_copies:
+        copy.start()
+    head_part(0, store_own)
+    for i, rows in ((0, top), (1, low)):
+        head_ring[i].wait_recv()
+
+        @pl.loop(0, steps)
+        def _(j):
+            columns = pl.ds(pl.multiple_of(j * step, step), step)
+            sent[i, rows, columns] = (
+                kept[i, :, columns] + relay[i, :, columns].astype(jnp.float32)
+            ).astype(jnp.bfloat16)
+
+        head_ring[4 + i].start()
+    total = squares_ref[chip]
+    for i, copy in enumerate(square_copies):
+        copy.wait_recv()
+        total += squares[i]
+    inverse = lax.rsqrt(total[:, :1] / features + 1e-06)
+    for load in loads[2:]:
+        load.wait()
+    for i in range(2, 6):
+        head_ring[i].wait_recv()
+
+    lanes = 128
+    lane = lax.broadcasted_iota(jnp.int32, (half, lanes), 1)
+    start = v * vocab
+
+    for part in (top, low):
+        scale = inverse[part.start : part.start + half]
+        target = ids_ref[part, :][:, :1] - start
+
+        def largest(j, carry):
+            at = pl.ds(pl.multiple_of(j * lanes, lanes), lanes)
+            value = (
+                logits[part, at]
+                + final[0, part, at].astype(jnp.float32)
+                + final[1, part, at].astype(jnp.float32)
+            ) * scale
+            logits[part, at] = value
+            return jnp.maximum(carry[0], value), jnp.maximum(carry[1], student[part, at])
+
+        lowest = jnp.full((half, lanes), -jnp.inf, jnp.float32)
+        teacher_max, student_max = lax.fori_loop(0, vocab // lanes, largest, (lowest, lowest))
+        teacher_max = jnp.max(teacher_max, axis=1, keepdims=True)
+        student_max = jnp.max(student_max, axis=1, keepdims=True)
+
+        def sums(j, carry):
+            at = pl.ds(pl.multiple_of(j * lanes, lanes), lanes)
+            teacher, own = logits[part, at], student[part, at]
+            weight = jnp.exp(own - student_max)
+            picked = lane + j * lanes == target
+            return (
+                carry[0] + jnp.exp(teacher - teacher_max),
+                carry[1] + weight,
+                carry[2] + weight * (own - teacher),
+                carry[3] + jnp.where(picked, own, 0.0),
+                carry[4] + jnp.where(picked, teacher, 0.0),
+            )
+
+        totals = lax.fori_loop(
+            0, vocab // lanes, sums, (jnp.zeros((half, lanes), jnp.float32),) * 5
+        )
+        table = jnp.where(lane == 0, teacher_max, jnp.where(lane == 1, student_max, 0.0))
+        for i, total in enumerate(totals):
+            table = jnp.where(lane == i + 2, jnp.sum(total, axis=1, keepdims=True), table)
+        columns_stat[part, :] = table
+
+    stat[...] = jnp.transpose(columns_stat[...])[:8]
+
+    def stat_copy(k, sender):
+        return pltpu.make_async_remote_copy(
+            src_ref=stat,
+            dst_ref=stats.at[sender],
+            send_sem=stat_send.at[k],
+            recv_sem=stat_recv.at[k],
+            device_id=(t, lax.rem(v + k, 16)),
+            device_id_type=MESH,
+        )
+
+    @pl.loop(1, 16)
+    def _(k):
+        stat_copy(k, v).start()
+
+    stats[v] = stat[...]
+
+    @pl.loop(1, 16)
+    def _(k):
+        stat_copy(k, lax.rem(v - k + 16, 16)).wait()
+
+    every = [stats[:, pl.ds(i, 1), :] for i in range(7)]
+    teacher_max = jnp.max(every[0], axis=0)
+    student_max = jnp.max(every[1], axis=0)
+    teacher_sum = jnp.sum(every[2] * jnp.exp(every[0] - teacher_max), axis=0)
+    student_scale = jnp.exp(every[1] - student_max)
+    student_sum = jnp.sum(every[3] * student_scale, axis=0)
+    expect = jnp.sum(every[4] * student_scale, axis=0) / student_sum
+    teacher_norm = teacher_max + jnp.log(teacher_sum)
+    student_norm = student_max + jnp.log(student_sum)
+    loss_ref[...] = (
+        expect
+        - student_norm
+        + teacher_norm
+        + (jnp.sum(every[5], axis=0) - student_norm)
+        - (jnp.sum(every[6], axis=0) - teacher_norm)
+    )
+    sublane = lax.broadcasted_iota(jnp.int32, (lanes, lanes), 0)
+    columns_stat[...] = jnp.transpose(
+        jnp.where(sublane == 0, student_norm, jnp.where(sublane == 1, expect, 0.0))
+    )
+    for part in (top, low):
+        norm = columns_stat[part, :][:, 0:1]
+        mean = columns_stat[part, :][:, 1:2]
+        scale = weight_ref[part, :][:, :1]
+        target = ids_ref[part, :][:, :1] - start
+
+        @pl.loop(0, vocab // lanes)
+        def _(j):
+            at = pl.ds(pl.multiple_of(j * lanes, lanes), lanes)
+            own = student[part, at]
+            prob = jnp.exp(own - norm)
+            picked = (lane + j * lanes == target).astype(jnp.float32)
+            grads[part, at] = (
+                scale * (prob * (own - logits[part, at] - mean) + picked - prob)
+            ).astype(jnp.bfloat16)
+
+    for copy in square_copies:
+        copy.wait_send()
+    for copy in head_ring:
+        copy.wait_send()
+
     plan = (
-        (g_ref.at[top], blocks.at[0, top], right),
-        (g_ref.at[low], blocks.at[0, low], right),
-        (g_ref.at[low], blocks.at[1, low], left),
-        (g_ref.at[top], blocks.at[1, top], left),
+        (grads.at[top], blocks.at[0, top], right),
+        (grads.at[low], blocks.at[0, low], right),
+        (grads.at[low], blocks.at[1, low], left),
+        (grads.at[top], blocks.at[1, top], left),
         (blocks.at[0, top], blocks.at[2, top], right),
         (blocks.at[1, low], blocks.at[2, low], left),
     )
@@ -285,8 +501,6 @@
     ]
     for i in (0, 2, 1, 3):
         ring[i].start()
-    for load in loads:
-        load.wait()
 
     def term_copy(slot, side, h, piece):
         return pltpu.make_async_remote_copy(
@@ -320,7 +534,7 @@
                     pl.when(piece != v)(term_copy(slot, side, h, piece).start)
                     pl.when(piece == v)(self_copy(slot, h).start)
 
-    multiply(0, g_ref)
+    multiply(0, grads)
     ring[0].wait_recv()
     ring[4].start()
     ring[2].wait_recv()
@@ -361,199 +575,57 @@
     out_ref[...] = total.astype(out_ref.dtype)
 
 
-def grad_reduce(logit_grad, head_own, head_pair, collective_id):
-    rows, columns = logit_grad.shape
-    width = head_own.shape[0]
+def loss_and_grad(
+    rows, squares, ids, weight, head_own, head_pair, own, pair, student, collective_id
+):
+    _, count, _ = rows.shape
+    width, vocab = head_own.shape
+    vmem = pl.BlockSpec(memory_space=pltpu.VMEM)
+    hbm = pl.BlockSpec(memory_space=pl.ANY)
+    bf16, f32 = jnp.bfloat16, jnp.float32
+    dma = pltpu.SemaphoreType.DMA
     return pl.pallas_call(
-        grad_kernel,
-        out_shape=jax.ShapeDtypeStruct((rows // 2, width), jnp.bfloat16),
-        in_specs=[
-            pl.BlockSpec(memory_space=pltpu.VMEM),
-            pl.BlockSpec(memory_space=pl.ANY),
-            pl.BlockSpec(memory_space=pl.ANY),
-        ],
-        out_specs=pl.BlockSpec(memory_space=pltpu.VMEM),
-        scratch_shapes=[
-            pltpu.VMEM((width, columns), jnp.bfloat16),
-            pltpu.VMEM((width, columns), jnp.bfloat16),
-            pltpu.VMEM((3, rows, columns), jnp.bfloat16),
-            pltpu.VMEM((4, 2, rows, width), jnp.bfloat16),
-            pltpu.VMEM((16, rows // 2, width), jnp.bfloat16),
-            pltpu.SemaphoreType.DMA((2,)),
-            pltpu.SemaphoreType.DMA((6,)),
-            pltpu.SemaphoreType.DMA((6,)),
-            pltpu.SemaphoreType.DMA((16,)),
-            pltpu.SemaphoreType.DMA((16,)),
-            pltpu.SemaphoreType.DMA,
+        loss_kernel,
+        out_shape=(
+            jax.ShapeDtypeStruct((1, count), f32),
+            jax.ShapeDtypeStruct((count // 2, width), bf16),
+        ),
+        in_specs=[vmem] * 4 + [hbm] * 5,
+        out_specs=(vmem, vmem),
+        scratch_shapes=[pltpu.VMEM((width, vocab), bf16)] * 4
+        + [
+            pltpu.VMEM((count, vocab), f32),
+            pltpu.VMEM((count, vocab), bf16),
+            pltpu.VMEM((2, count // 2, vocab), f32),
+            pltpu.VMEM((2, count // 2, vocab), bf16),
+            pltpu.VMEM((2, count, vocab), bf16),
+            pltpu.VMEM((2, count, vocab), bf16),
+            pltpu.VMEM((3, count, 128), f32),
+            pltpu.VMEM((count, vocab), f32),
+            pltpu.VMEM((count, 128), f32),
+            pltpu.VMEM((8, count), f32),
+            pltpu.VMEM((16, 8, count), f32),
+            pltpu.VMEM((count, vocab), bf16),
+            pltpu.VMEM((3, count, vocab), bf16),
+            pltpu.VMEM((4, 2, count, width), bf16),
+            pltpu.VMEM((16, count // 2, width), bf16),
+            dma((5,)),
+            dma((6,)),
+            dma((6,)),
+            dma((3,)),
+            dma((3,)),
+            dma((16,)),
+            dma((16,)),
+            dma((6,)),
+            dma((6,)),
+            dma((16,)),
+            dma((16,)),
+            dma,
         ],
         compiler_params=pltpu.CompilerParams(
-            collective_id=collective_id, has_side_effects=True, vmem_limit_bytes=56 * 1024 * 1024
+            collective_id=collective_id, has_side_effects=True, vmem_limit_bytes=60 * 1024 * 1024
         ),
-    )(logit_grad, head_own, head_pair)
-
-
-def head_kernel(
-    rows_ref, squares_ref, own_hbm, pair_hbm, out_ref,
-    own_w, pair_w, far, kept, relay, sent, final, squares,
-    load_sem, ring_send, ring_recv, square_send, square_recv,
-):
-    t, v = lax.axis_index("tok"), lax.axis_index("voc")
-    core = lax.rem(t, 2)
-    chip = t // 2
-    right, left, across = lax.rem(t + 2, 8), lax.rem(t + 6, 8), lax.rem(t + 4, 8)
-    half = rows_ref.shape[1] // 2
-    width = own_w.shape[0]
-    features = rows_ref.shape[2] * 4
-    loads = (
-        pltpu.make_async_copy(own_hbm, own_w, load_sem.at[0]),
-        pltpu.make_async_copy(pair_hbm, pair_w, load_sem.at[1]),
-    )
-    for load in loads:
-        load.start()
-    barrier = pltpu.get_barrier_semaphore()
-    for side in (right, left, across):
-        pl.semaphore_signal(barrier, inc=1, device_id=(side, v), device_id_type=MESH)
-    pl.semaphore_wait(barrier, 3)
-
-    chips = [lax.rem(chip + shift, 4) for shift in range(4)]
-    square_copies = [
-        pltpu.make_async_remote_copy(
-            src_ref=squares_ref.at[chips[shift]],
-            dst_ref=squares.at[shift - 1],
-            send_sem=square_send.at[shift - 1],
-            recv_sem=square_recv.at[shift - 1],
-            device_id=(device, v),
-            device_id_type=MESH,
-        )
-        for shift, device in ((1, right), (2, across), (3, left))
-    ]
-    top, low = pl.ds(0, half), pl.ds(half, half)
-    plan = (
-        (far.at[top], relay.at[0], right),
-        (far.at[low], relay.at[1], left),
-        (sent.at[0, low], final.at[0, low], right),
-        (sent.at[1, top], final.at[1, top], left),
-        (sent.at[0, top], final.at[0, top], right),
-        (sent.at[1, low], final.at[1, low], left),
-    )
-    ring = [
-        pltpu.make_async_remote_copy(
-            src_ref=source,
-            dst_ref=target,
-            send_sem=ring_send.at[i],
-            recv_sem=ring_recv.at[i],
-            device_id=(device, v),
-            device_id_type=MESH,
-        )
-        for i, (source, target, device) in enumerate(plan)
-    ]
-    own_columns = pl.ds(pl.multiple_of(core * width, width), width)
-    pair_columns = pl.ds(pl.multiple_of((1 - core) * width, width), width)
-    step = 256
-    steps = own_w.shape[1] // step
-
-    def multiply(shift, store):
-        own_rows = rows_ref[chips[shift], :, own_columns]
-        pair_rows = rows_ref[chips[shift], :, pair_columns]
-
-        @pl.loop(0, steps)
-        def _(j):
-            columns = pl.ds(pl.multiple_of(j * step, step), step)
-            store(
-                columns,
-                jnp.dot(own_rows, own_w[:, columns], preferred_element_type=jnp.float32)
-                + jnp.dot(pair_rows, pair_w[:, columns], preferred_element_type=jnp.float32),
-            )
-
-    def store_far(columns, value):
-        far[:, columns] = value.astype(jnp.bfloat16)
-
-    def store_right(columns, value):
-        kept[0, :, columns] = value[:half]
-        sent[0, low, columns] = value[half:].astype(jnp.bfloat16)
-
-    def store_left(columns, value):
-        kept[1, :, columns] = value[half:]
-        sent[1, top, columns] = value[:half].astype(jnp.bfloat16)
-
-    def store_own(columns, value):
-        out_ref[:, columns] = value
-
-    for load in loads:
-        load.wait()
-    multiply(2, store_far)
-    ring[0].start()
-    ring[1].start()
-    multiply(1, store_right)
-    ring[2].start()
-    multiply(3, store_left)
-    ring[3].start()
-    for copy in square_copies:
-        copy.start()
-    multiply(0, store_own)
-    for i, rows in ((0, top), (1, low)):
-        ring[i].wait_recv()
-
-        @pl.loop(0, steps)
-        def _(j):
-            columns = pl.ds(pl.multiple_of(j * step, step), step)
-            sent[i, rows, columns] = (
-                kept[i, :, columns] + relay[i, :, columns].astype(jnp.float32)
-            ).astype(jnp.bfloat16)
-
-        ring[4 + i].start()
-    total = squares_ref[chip]
-    for i, copy in enumerate(square_copies):
-        copy.wait_recv()
-        total += squares[i]
-    inverse = lax.rsqrt(total[:, :1] / features + 1e-06)
-    for i in range(2, 6):
-        ring[i].wait_recv()
-
-    @pl.loop(0, steps)
-    def _(j):
-        columns = pl.ds(pl.multiple_of(j * step, step), step)
-        out_ref[:, columns] = (
-            out_ref[:, columns]
-            + final[0, :, columns].astype(jnp.float32)
-            + final[1, :, columns].astype(jnp.float32)
-        ) * inverse
-
-    for copy in square_copies:
-        copy.wait_send()
-    for copy in ring:
-        copy.wait_send()
-
-
-def head_reduce(rows, squares, head_own, head_pair, collective_id):
-    chips, count, _ = rows.shape
-    width, columns = head_own.shape
-    vmem = pl.BlockSpec(memory_space=pltpu.VMEM)
-    hbm = pl.BlockSpec(memory_space=pl.ANY)
-    return pl.pallas_call(
-        head_kernel,
-        out_shape=jax.ShapeDtypeStruct((count, columns), jnp.float32),
-        in_specs=[vmem, vmem, hbm, hbm],
-        out_specs=vmem,
-        scratch_shapes=[
-            pltpu.VMEM((width, columns), jnp.bfloat16),
-            pltpu.VMEM((width, columns), jnp.bfloat16),
-            pltpu.VMEM((count, columns), jnp.bfloat16),
-            pltpu.VMEM((2, count // 2, columns), jnp.float32),
-            pltpu.VMEM((2, count // 2, columns), jnp.bfloat16),
-            pltpu.VMEM((2, count, columns), jnp.bfloat16),
-            pltpu.VMEM((2, count, columns), jnp.bfloat16),
-            pltpu.VMEM((3, count, 128), jnp.float32),
-            pltpu.SemaphoreType.DMA((2,)),
-            pltpu.SemaphoreType.DMA((6,)),
-            pltpu.SemaphoreType.DMA((6,)),
-            pltpu.SemaphoreType.DMA((3,)),
-            pltpu.SemaphoreType.DMA((3,)),
-        ],
-        compiler_params=pltpu.CompilerParams(
-            collective_id=collective_id, has_side_effects=True, vmem_limit_bytes=56 * 1024 * 1024
-        ),
-    )(rows, squares, head_own, head_pair)
+    )(rows, squares, ids, weight, head_own, head_pair, own, pair, student)
 
 
 def per_device(
@@ -669,54 +741,20 @@
         8,
         targets=(at_second, at_second),
     )
-    vocab_local = teacher_head.shape[1]
-    teacher_logits = head_reduce(
-        teacher_rows.reshape(chips, voc_count * rows_here, chip_width),
-        squares_rows.reshape(chips, voc_count * rows_here, 128),
+    token_count = sampled_ids.shape[0]
+    token_loss, hidden_grad = loss_and_grad(
+        teacher_rows.reshape(chips, token_count, chip_width),
+        squares_rows.reshape(chips, token_count, 128),
+        jnp.broadcast_to(sampled_ids[:, None], (token_count, 128)),
+        jnp.broadcast_to(token_weight[:, None], (token_count, 128)),
         teacher_head,
         teacher_pair,
+        student_head,
+        student_pair,
+        student_logits,
         10,
     )
-    differ = student_logits - teacher_logits
-    vocab_start = lax.axis_index("voc") * vocab_local
-    picked = sampled_ids[:, None] - vocab_start == jnp.arange(vocab_local, dtype=jnp.int32)[None, :]
-    local_tmax = jnp.max(teacher_logits, axis=1)
-    local_smax = jnp.max(student_logits, axis=1)
-    student_exp = jnp.exp(student_logits - local_smax[:, None])
-    stats = jnp.stack(
-        [
-            local_tmax,
-            local_smax,
-            jnp.sum(jnp.exp(teacher_logits - local_tmax[:, None]), axis=1),
-            jnp.sum(student_exp, axis=1),
-            jnp.sum(student_exp * differ, axis=1),
-            jnp.sum(jnp.where(picked, student_logits, 0.0), axis=1),
-            jnp.sum(jnp.where(picked, teacher_logits, 0.0), axis=1),
-            jnp.zeros_like(local_tmax),
-        ]
-    )
-    (every,) = exchange([stats], [(voc_count,) + stats.shape], ("voc",), 9)
-    teacher_max = jnp.max(every[:, 0], axis=0)
-    student_max = jnp.max(every[:, 1], axis=0)
-    teacher_scale = jnp.exp(every[:, 0] - teacher_max[None, :])
-    student_scale = jnp.exp(every[:, 1] - student_max[None, :])
-    teacher_sum = jnp.sum(every[:, 2] * teacher_scale, axis=0)
-    student_sum = jnp.sum(every[:, 3] * student_scale, axis=0)
-    cross_sum = jnp.sum(every[:, 4] * student_scale, axis=0)
-    picked_s = jnp.sum(every[:, 5], axis=0)
-    picked_t = jnp.sum(every[:, 6], axis=0)
-    teacher_norm = teacher_max + jnp.log(teacher_sum)
-    student_norm = student_max + jnp.log(student_sum)
-    expect = cross_sum / student_sum
-    token_loss = (
-        expect - student_norm + teacher_norm + (picked_s - student_norm) - (picked_t - teacher_norm)
-    )
-    student_prob = jnp.exp(student_logits - student_norm[:, None])
-    logit_grad = (
-        token_weight[:, None]
-        * (student_prob * (differ - expect[:, None]) + picked.astype(jnp.float32) - student_prob)
-    ).astype(jnp.bfloat16)
-    hidden_grad = grad_reduce(logit_grad, student_head, student_pair, 4)
+    token_loss = token_loss.reshape(token_count)
     return (token_loss, hidden_grad)
 
 

time: 316 us -> 315 us (level)
  other arithmetic: 22.9 us -> 7.53 us
  Pallas kernels: 253 us -> 264 us
    pallas_call x2 -> x1, Pallas kernels: 122 us -> 141 us  [loss_and_grad(): pl.pallas_call(loss_kernel, out_shape=(jax.ShapeDtypeStruct((1, count), f...]
    pallas_call x4 -> x3, Pallas kernels: 74.3 us -> 65.5 us  [exchange(): pl.pallas_call(functools.partial(exchange_kernel, axes, sizes, source, ta...]
    reduce_sum x3 -> x0, other arithmetic: 5.02 us -> none  [the longest x1 4.97 us: per_device(): jnp.sum(student_exp * differ, axis=1)]
    convert_element_type x1 -> x0, other arithmetic: 4.58 us -> none  [per_device(): logit_grad = (token_weight[:, None] * (student_prob * (differ - expect[:,...]
    reduce_max x4 -> x0, other arithmetic: 3.98 us -> none  [the longest x1 2.05 us: per_device(): local_tmax = jnp.max(teacher_logits, axis=1)]
  transfers between devices with their start and end apart: 3 -> 3, of which waited for: 0 -> 1; matrix products, arithmetic and copies ran while one was open for 8% -> 3% of each run, Pallas kernels for 53% -> 32%
where the time goes in v5:
time: 315 us
  Pallas kernels  264 us (84%)
  matrix products  17.1 us (5%)
  between operations  14.2 us (5%)
  local copies, waits for them, and re-layouts  7.57 us (2%)
  other arithmetic  7.53 us (2%)
    pallas_call x1, Pallas kernels, loss_and_grad(): pl.pallas_call(loss_kernel, out_shape=(jax.ShapeDtypeStruct((1, count), f...  141 us
    pallas_call x3, Pallas kernels, exchange(): pl.pallas_call(functools.partial(exchange_kernel, axes, sizes, source, ta...  65.5 us
    pallas_call x1, Pallas kernels, expert_layer(): pl.pallas_call(expert_kernel, out_shape=jax.ShapeDtypeStruct((16, group,...  57.6 us
    dot_general x1, matrix products, per_device(): jnp.dot(student_all.reshape(-1, part_width), student_head, preferred_elem...  12.1 us
  transfers between devices with their start and end apart: 3, of which 1 were waited for; matrix products, arithmetic and copies ran while one was open for 3% of the time, Pallas kernels for 32%

profile of v5, /device:TPU:17, one launch (start us, length us, event | category | flops | bytes accessed | tf_op | source)
XLA Modules:
  0.0 314.5 jit_solution(6466801718937455330)
XLA Ops:
  7.2 0.7 convert_element_type.43
  7.9 0.1 pad.2.clone
  8.0 1.4 maximum_maximum_fusion.refs_2_
  9.4 22.0 %shard_map.131 = (bf16[16,64,512]{2,1,0:T(8,128)(2,1)}, bf16[8,8,4096]{2,1,0:T(8,128)(2,1)}, f32[8,8,128]{2,1,0:T(8,128)}) custom-call(bf16[64,512]{1,0:T(8,128)(2,1)} %refs_0_.1, bf16[8,4096]{1,0:T(8,128)(2,1)} %refs_1_.1, f32[8,128]{1,0:T(8,128)} %maximum_maximum_fusion.refs_2_), custom_call_target="tpu_custom_call" | custom-call | tf_op jit(solution)/shard_map/pallas_call | solution.py:92
  31.4 1.3 fusion.50
  32.7 0.1 copy.23
  32.8 0.1 copy.24
  32.9 0.1 copy.25
  33.0 0.1 copy.26
  33.2 0.1 copy.30
  33.3 0.3 fusion.1
  33.7 2.5 convolution_convert_fusion
  36.2 12.1 %fusion.51 = f32[1024,4864]{1,0:T(8,128)} fusion(bf16[1024,512]{1,0:T(8,128)(2,1)} %bitcast.66, bf16[512,4864]{1,0:T(8,128)(2,1)} %own_hbm.1), kind=kOutput, calls=%fused_computation.98 | convolution fusion | flops 5100273664 | bytes 25952256 | tf_op jit(solution)/shard_map/dot_general | solution.py:668
  48.3 1.6 collective-permute-start
  49.9 0.3 collective-permute-start.1
  50.2 0.2 slice_reduce_fusion
  50.4 57.6 %shard_map.132 = bf16[16,16,4096]{2,1,0:T(8,128)(2,1)} custom-call(bf16[8,16,4096]{2,1,0:T(8,128)(2,1)} %bitcast.44, bf16[4096,384]{1,0:T(8,128)(2,1)} %gate_hbm.1, bf16[4096,384]{1,0:T(8,128)(2,1)} %up_hbm.1, bf16[384,4096]{1,0:T(8,128)(2,1)} %down_hbm.1), custom_call_target="tpu_custom_call" | custom-call | tf_op jit(solution)/shard_map/pallas_call | solution.py:203
  108.0 2.5 convert_reduce_fusion
  110.6 2.1 convolution_convert_fusion.1.refs_0_
  112.8 16.8 %shard_map.133 = bf16[8,32,1024]{2,1,0:T(8,128)(2,1)} custom-call(bf16[64,4096]{1,0:T(8,128)(2,1)} %convolution_convert_fusion.1.refs_0_), custom_call_target="tpu_custom_call" | custom-call | tf_op jit(solution)/shard_map/pallas_call | solution.py:92
  129.6 0.7 dynamic_slice.7
  130.3 1.1 convert_reduce_fusion.1
  131.5 1.6 multiply_reduce_fusion
  133.1 0.1 broadcast_in_dim.130
  133.2 0.7 broadcast_in_dim.131.refs_1_
  133.9 26.6 %shard_map.134 = (bf16[4,16,8,1024]{3,2,1,0:T(8,128)(2,1)}, f32[4,16,8,128]{3,2,1,0:T(8,128)}) custom-call(bf16[4,8,1024]{2,1,0:T(8,128)(2,1)} %get-tuple-element.21.refs_0_, f32[4,8,128]{2,1,0:T(8,128)} %broadcast_in_dim.131.refs_1_), custom_call_target="tpu_custom_call" | custom-call | tf_op jit(solution)/shard_map/pallas_call | solution.py:92
  160.5 2.5 reduce-scatter.2.cloned.1.call-done.student_hbm
  163.0 0.7 broadcast_in_dim.132.ids_ref
  163.7 0.7 broadcast_in_dim.133.weight_ref
  164.4 140.6 %shard_map.135 = (f32[1,128]{1,0:T(1,128)}, bf16[64,512]{1,0:T(8,128)(2,1)}) custom-call(bf16[4,128,1024]{2,1,0:T(8,128)(2,1)} %bitcast.47, f32[4,128,128]{2,1,0:T(8,128)} %bitcast.49, s32[128,128]{1,0:T(8,128)} %broadcast_in_dim.132.ids_ref, f32[128,128]{1,0:T(8,128)} %broadcast_in_dim.133.weight_ref, bf16[512,4864]{1,0:T(8,128)(2,1)} %head_own_hbm.1, ...), custom_call_target="tpu_custom_call" | custom-call | tf_op jit(solution)/shard_map/pallas_call | solution.py:587
  305.0 1.2 copy.38
  306.2 1.5 copy.39
  (20 shorter events, 0.4 us)
Async XLA Ops:
  7.2 155.8 %reduce-scatter.2.cloned.1.call-start = ((), (), s32[]{:S(2)}) async-start(), calls=%async_computation.1 | async-start | bytes 22413312 | tf_op jit(solution)/shard_map/reduce_scatter | solution.py:705
  48.3 1.9 copy-start
  48.3 112.2 %collective-permute-start = (bf16[512,4864]{1,0:T(8,128)(2,1)}, bf16[512,4864]{1,0:T(8,128)(2,1)}, u32[]{:S(2)}, u32[]{:S(2)}) collective-permute-start(bf16[512,4864]{1,0:T(8,128)(2,1)} %head_own_hbm.1), channel_id=1, source_target_pairs={{0,16},{16,0},{32,48},{48,32},{64,80},{80,64},{96,112},{112,96},{1... | collective-permute-start | bytes 14942216 | tf_op jit(solution)/shard_map/ppermute | solution.py:651
  49.9 110.6 %collective-permute-start.1 = (bf16[512,4864]{1,0:T(8,128)(2,1)}, bf16[512,4864]{1,0:T(8,128)(2,1)}, u32[]{:S(2)}, u32[]{:S(2)}) collective-permute-start(bf16[512,4864]{1,0:T(8,128)(2,1)} %own_hbm.1), channel_id=1, source_target_pairs={{0,16},{16,0},{32,48},{48,32},{64,80},{80,64},{96,112},{112,96},{1... | collective-permute-start | bytes 14942216 | tf_op jit(solution)/shard_map/ppermute | solution.py:650
  110.6 52.4 %copy-start.1 = (s32[128]{0:T(128)S(1)}, s32[128]{0:T(128)}, u32[]{:S(2)}) copy-start(s32[128]{0:T(128)} %param.22) | copy-start | bytes 1540
  110.6 53.1 %copy-start.2 = (f32[128]{0:T(128)S(1)}, f32[128]{0:T(128)}, u32[]{:S(2)}) copy-start(f32[128]{0:T(128)} %param.23) | copy-start | bytes 1540
Sparse Core Ops, SparseCore 0:
  48.4 114.5 reduce-scatter.1

commit v6 on v5

--- a/solution.py
+++ b/solution.py
@@ -228,7 +228,7 @@
     rows_ref, squares_ref, ids_ref, weight_ref,
     head_own_hbm, head_pair_hbm, own_hbm, pair_hbm, student_hbm,
     loss_ref, out_ref,
-    head_own, head_pair, own_w, pair_w, student,
+    head_w, own_w, pair_w, student, expo,
     far, kept, relay, sent, final, squares, logits,
     columns_stat, stat, stats, grads, blocks, terms, landed,
     load_sem, head_send, head_recv, square_send, square_recv, stat_send, stat_recv,
@@ -251,8 +251,11 @@
         pltpu.make_async_copy(source, target, load_sem.at[i])
         for i, (source, target) in enumerate(
             (
-                (head_own_hbm, head_own),
-                (head_pair_hbm, head_pair),
+                (head_own_hbm, head_w.at[pl.ds(pl.multiple_of(core * width, width), width)]),
+                (
+                    head_pair_hbm,
+                    head_w.at[pl.ds(pl.multiple_of((1 - core) * width, width), width)],
+                ),
                 (student_hbm, student),
                 (own_hbm, own_w),
                 (pair_hbm, pair_w),
@@ -308,21 +311,13 @@
         )
         for i, (source, target, device) in enumerate(head_plan)
     ]
-    own_columns = pl.ds(pl.multiple_of(core * width, width), width)
-    pair_columns = pl.ds(pl.multiple_of((1 - core) * width, width), width)
-
     def head_part(shift, store):
-        own_rows = rows_ref[chips[shift], :, own_columns]
-        pair_rows = rows_ref[chips[shift], :, pair_columns]
+        block = rows_ref[chips[shift]]
 
         @pl.loop(0, steps)
         def _(j):
             columns = pl.ds(pl.multiple_of(j * step, step), step)
-            store(
-                columns,
-                jnp.dot(own_rows, head_own[:, columns], preferred_element_type=jnp.float32)
-                + jnp.dot(pair_rows, head_pair[:, columns], preferred_element_type=jnp.float32),
-            )
+            store(columns, jnp.dot(block, head_w[:, columns], preferred_element_type=jnp.float32))
 
     def store_far(columns, value):
         far[:, columns] = value.astype(jnp.bfloat16)
@@ -370,51 +365,76 @@
     inverse = lax.rsqrt(total[:, :1] / features + 1e-06)
     for load in loads[2:]:
         load.wait()
-    for i in range(2, 6):
-        head_ring[i].wait_recv()
-
     lanes = 128
     lane = lax.broadcasted_iota(jnp.int32, (half, lanes), 1)
     start = v * vocab
-
+    lowest = jnp.full((half, lanes), -jnp.inf, jnp.float32)
+    nothing = jnp.zeros((half, lanes), jnp.float32)
+
+    def sweep(body, carry):
+        def pair(j, carry):
+            for u in range(2):
+                first = j * 2 * lanes + u * lanes
+                carry = body(pl.ds(pl.multiple_of(first, lanes), lanes), first, carry)
+            return carry
+
+        return lax.fori_loop(0, vocab // (2 * lanes), pair, carry)
+
+    def row_sum(value):
+        return jnp.sum(value, axis=1, keepdims=True)
+
+    student_side = []
     for part in (top, low):
+        target = ids_ref[part, :][:, :1] - start
+        student_max = jnp.max(
+            sweep(lambda at, first, carry: jnp.maximum(carry, student[part, at]), lowest),
+            axis=1,
+            keepdims=True,
+        )
+
+        def student_sums(at, first, carry):
+            own = student[part, at]
+            weight = jnp.exp(own - student_max)
+            expo[part, at] = weight
+            return carry[0] + weight, carry[1] + jnp.where(lane + first == target, own, 0.0)
+
+        total, picked = sweep(student_sums, (nothing, nothing))
+        student_side.append((target, student_max, row_sum(total), row_sum(picked)))
+
+    for i in range(2, 6):
+        head_ring[i].wait_recv()
+
+    for index, part in enumerate((top, low)):
         scale = inverse[part.start : part.start + half]
-        target = ids_ref[part, :][:, :1] - start
-
-        def largest(j, carry):
-            at = pl.ds(pl.multiple_of(j * lanes, lanes), lanes)
+        target, student_max, student_sum, student_picked = student_side[index]
+
+        def largest(at, first, carry):
             value = (
                 logits[part, at]
                 + final[0, part, at].astype(jnp.float32)
                 + final[1, part, at].astype(jnp.float32)
             ) * scale
             logits[part, at] = value
-            return jnp.maximum(carry[0], value), jnp.maximum(carry[1], student[part, at])
-
-        lowest = jnp.full((half, lanes), -jnp.inf, jnp.float32)
-        teacher_max, student_max = lax.fori_loop(0, vocab // lanes, largest, (lowest, lowest))
-        teacher_max = jnp.max(teacher_max, axis=1, keepdims=True)
-        student_max = jnp.max(student_max, axis=1, keepdims=True)
-
-        def sums(j, carry):
-            at = pl.ds(pl.multiple_of(j * lanes, lanes), lanes)
-            teacher, own = logits[part, at], student[part, at]
-            weight = jnp.exp(own - student_max)
-            picked = lane + j * lanes == target
+            return jnp.maximum(carry, value)
+
+        teacher_max = jnp.max(sweep(largest, lowest), axis=1, keepdims=True)
+
+        def sums(at, first, carry):
+            teacher = logits[part, at]
             return (
                 carry[0] + jnp.exp(teacher - teacher_max),
-                carry[1] + weight,
-                carry[2] + weight * (own - teacher),
-                carry[3] + jnp.where(picked, own, 0.0),
-                carry[4] + jnp.where(picked, teacher, 0.0),
+                carry[1] + expo[part, at] * (student[part, at] - teacher),
+                carry[2] + jnp.where(lane + first == target, teacher, 0.0),
             )
 
-        totals = lax.fori_loop(
-            0, vocab // lanes, sums, (jnp.zeros((half, lanes), jnp.float32),) * 5
-        )
-        table = jnp.where(lane == 0, teacher_max, jnp.where(lane == 1, student_max, 0.0))
-        for i, total in enumerate(totals):
-            table = jnp.where(lane == i + 2, jnp.sum(total, axis=1, keepdims=True), table)
+        teacher_sum, cross, teacher_picked = [
+            row_sum(total) for total in sweep(sums, (nothing,) * 3)
+        ]
+        table = jnp.where(lane == 0, teacher_max, 0.0)
+        for i, column in enumerate(
+            (student_max, teacher_sum, student_sum, cross, student_picked, teacher_picked)
+        ):
+            table = jnp.where(lane == i + 1, column, table)
         columns_stat[part, :] = table
 
     stat[...] = jnp.transpose(columns_stat[...])[:8]
@@ -459,21 +479,22 @@
     columns_stat[...] = jnp.transpose(
         jnp.where(sublane == 0, student_norm, jnp.where(sublane == 1, expect, 0.0))
     )
-    for part in (top, low):
+    for index, part in enumerate((top, low)):
         norm = columns_stat[part, :][:, 0:1]
         mean = columns_stat[part, :][:, 1:2]
         scale = weight_ref[part, :][:, :1]
-        target = ids_ref[part, :][:, :1] - start
-
-        @pl.loop(0, vocab // lanes)
-        def _(j):
-            at = pl.ds(pl.multiple_of(j * lanes, lanes), lanes)
-            own = student[part, at]
-            prob = jnp.exp(own - norm)
-            picked = (lane + j * lanes == target).astype(jnp.float32)
+        target, local_max, _, _ = student_side[index]
+        factor = jnp.exp(local_max - norm)
+
+        def gradient(at, first, carry):
+            prob = expo[part, at] * factor
+            picked = (lane + first == target).astype(jnp.float32)
             grads[part, at] = (
-                scale * (prob * (own - logits[part, at] - mean) + picked - prob)
+                scale * (prob * (student[part, at] - logits[part, at] - mean) + picked - prob)
             ).astype(jnp.bfloat16)
+            return carry
+
+        sweep(gradient, 0)
 
     for copy in square_copies:
         copy.wait_send()
@@ -592,8 +613,11 @@
         ),
         in_specs=[vmem] * 4 + [hbm] * 5,
         out_specs=(vmem, vmem),
-        scratch_shapes=[pltpu.VMEM((width, vocab), bf16)] * 4
-        + [
+        scratch_shapes=[
+            pltpu.VMEM((2 * width, vocab), bf16),
+            pltpu.VMEM((width, vocab), bf16),
+            pltpu.VMEM((width, vocab), bf16),
+            pltpu.VMEM((count, vocab), f32),
             pltpu.VMEM((count, vocab), f32),
             pltpu.VMEM((count, vocab), bf16),
             pltpu.VMEM((2, count // 2, vocab), f32),

time: 315 us -> 305 us (0.968)
  Pallas kernels: 264 us -> 254 us
    pallas_call x1, Pallas kernels: 141 us -> 131 us  [loss_and_grad(): pl.pallas_call(loss_kernel, out_shape=(jax.ShapeDtypeStruct((1, count), f...]
  transfers between devices with their start and end apart: 3 -> 3, of which waited for: 1 -> 1; matrix products, arithmetic and copies ran while one was open for 3% -> 3% of each run, Pallas kernels for 32% -> 33%
where the time goes in v6:
time: 305 us
  Pallas kernels  254 us (83%)
  matrix products  17.1 us (6%)
  between operations  14.2 us (5%)
  local copies, waits for them, and re-layouts  7.57 us (2%)
  other arithmetic  7.53 us (2%)
    pallas_call x1, Pallas kernels, loss_and_grad(): pl.pallas_call(loss_kernel, out_shape=(jax.ShapeDtypeStruct((1, count), f...  131 us
    pallas_call x3, Pallas kernels, exchange(): pl.pallas_call(functools.partial(exchange_kernel, axes, sizes, source, ta...  65.5 us
    pallas_call x1, Pallas kernels, expert_layer(): pl.pallas_call(expert_kernel, out_shape=jax.ShapeDtypeStruct((16, group,...  57.6 us
    dot_general x1, matrix products, per_device(): jnp.dot(student_all.reshape(-1, part_width), student_head, preferred_elem...  12.1 us
  transfers between devices with their start and end apart: 3, of which 1 were waited for; matrix products, arithmetic and copies ran while one was open for 3% of the time, Pallas kernels for 33%

profile of v6, /device:TPU:17, one launch (start us, length us, event | category | flops | bytes accessed | tf_op | source)
XLA Modules:
  0.0 304.6 jit_solution(6404354928142472842)
XLA Ops:
  7.2 0.7 convert_element_type.43
  7.9 0.1 pad.2.clone
  8.0 1.4 maximum_maximum_fusion.refs_2_
  9.4 22.0 %shard_map.131 = (bf16[16,64,512]{2,1,0:T(8,128)(2,1)}, bf16[8,8,4096]{2,1,0:T(8,128)(2,1)}, f32[8,8,128]{2,1,0:T(8,128)}) custom-call(bf16[64,512]{1,0:T(8,128)(2,1)} %refs_0_.1, bf16[8,4096]{1,0:T(8,128)(2,1)} %refs_1_.1, f32[8,128]{1,0:T(8,128)} %maximum_maximum_fusion.refs_2_), custom_call_target="tpu_custom_call" | custom-call | tf_op jit(solution)/shard_map/pallas_call | solution.py:92
  31.4 1.3 fusion.50
  32.7 0.1 copy.23
  32.8 0.1 copy.24
  32.9 0.1 copy.25
  33.0 0.1 copy.26
  33.2 0.1 copy.30
  33.3 0.3 fusion.1
  33.7 2.5 convolution_convert_fusion
  36.2 12.1 %fusion.51 = f32[1024,4864]{1,0:T(8,128)} fusion(bf16[1024,512]{1,0:T(8,128)(2,1)} %bitcast.66, bf16[512,4864]{1,0:T(8,128)(2,1)} %own_hbm.1), kind=kOutput, calls=%fused_computation.98 | convolution fusion | flops 5100273664 | bytes 25952256 | tf_op jit(solution)/shard_map/dot_general | solution.py:692
  48.3 1.6 collective-permute-start
  49.9 0.3 collective-permute-start.1
  50.2 0.2 slice_reduce_fusion
  50.4 57.6 %shard_map.132 = bf16[16,16,4096]{2,1,0:T(8,128)(2,1)} custom-call(bf16[8,16,4096]{2,1,0:T(8,128)(2,1)} %bitcast.44, bf16[4096,384]{1,0:T(8,128)(2,1)} %gate_hbm.1, bf16[4096,384]{1,0:T(8,128)(2,1)} %up_hbm.1, bf16[384,4096]{1,0:T(8,128)(2,1)} %down_hbm.1), custom_call_target="tpu_custom_call" | custom-call | tf_op jit(solution)/shard_map/pallas_call | solution.py:203
  108.0 2.5 convert_reduce_fusion
  110.6 2.1 convolution_convert_fusion.1.refs_0_
  112.8 16.8 %shard_map.133 = bf16[8,32,1024]{2,1,0:T(8,128)(2,1)} custom-call(bf16[64,4096]{1,0:T(8,128)(2,1)} %convolution_convert_fusion.1.refs_0_), custom_call_target="tpu_custom_call" | custom-call | tf_op jit(solution)/shard_map/pallas_call | solution.py:92
  129.6 0.7 dynamic_slice.7
  130.3 1.1 convert_reduce_fusion.1
  131.5 1.6 multiply_reduce_fusion
  133.1 0.1 broadcast_in_dim.130
  133.2 0.7 broadcast_in_dim.131.refs_1_
  133.9 26.6 %shard_map.134 = (bf16[4,16,8,1024]{3,2,1,0:T(8,128)(2,1)}, f32[4,16,8,128]{3,2,1,0:T(8,128)}) custom-call(bf16[4,8,1024]{2,1,0:T(8,128)(2,1)} %get-tuple-element.21.refs_0_, f32[4,8,128]{2,1,0:T(8,128)} %broadcast_in_dim.131.refs_1_), custom_call_target="tpu_custom_call" | custom-call | tf_op jit(solution)/shard_map/pallas_call | solution.py:92
  160.5 2.5 reduce-scatter.2.cloned.1.call-done.student_hbm
  163.0 0.7 broadcast_in_dim.132.ids_ref
  163.7 0.7 broadcast_in_dim.133.weight_ref
  164.4 130.7 %shard_map.135 = (f32[1,128]{1,0:T(1,128)}, bf16[64,512]{1,0:T(8,128)(2,1)}) custom-call(bf16[4,128,1024]{2,1,0:T(8,128)(2,1)} %bitcast.47, f32[4,128,128]{2,1,0:T(8,128)} %bitcast.49, s32[128,128]{1,0:T(8,128)} %broadcast_in_dim.132.ids_ref, f32[128,128]{1,0:T(8,128)} %broadcast_in_dim.133.weight_ref, bf16[512,4864]{1,0:T(8,128)(2,1)} %head_own_hbm.1, ...), custom_call_target="tpu_custom_call" | custom-call | tf_op jit(solution)/shard_map/pallas_call | solution.py:608
  295.1 1.2 copy.38
  296.3 1.5 copy.39
  (20 shorter events, 0.4 us)
Async XLA Ops:
  7.2 155.8 %reduce-scatter.2.cloned.1.call-start = ((), (), s32[]{:S(2)}) async-start(), calls=%async_computation.1 | async-start | bytes 22413312 | tf_op jit(solution)/shard_map/reduce_scatter | solution.py:729
  48.3 1.9 copy-start
  48.3 112.2 %collective-permute-start = (bf16[512,4864]{1,0:T(8,128)(2,1)}, bf16[512,4864]{1,0:T(8,128)(2,1)}, u32[]{:S(2)}, u32[]{:S(2)}) collective-permute-start(bf16[512,4864]{1,0:T(8,128)(2,1)} %head_own_hbm.1), channel_id=1, source_target_pairs={{0,16},{16,0},{32,48},{48,32},{64,80},{80,64},{96,112},{112,96},{1... | collective-permute-start | bytes 14942216 | tf_op jit(solution)/shard_map/ppermute | solution.py:675
  49.9 110.6 %collective-permute-start.1 = (bf16[512,4864]{1,0:T(8,128)(2,1)}, bf16[512,4864]{1,0:T(8,128)(2,1)}, u32[]{:S(2)}, u32[]{:S(2)}) collective-permute-start(bf16[512,4864]{1,0:T(8,128)(2,1)} %own_hbm.1), channel_id=1, source_target_pairs={{0,16},{16,0},{32,48},{48,32},{64,80},{80,64},{96,112},{112,96},{1... | collective-permute-start | bytes 14942216 | tf_op jit(solution)/shard_map/ppermute | solution.py:674
  110.6 52.4 %copy-start.1 = (s32[128]{0:T(128)S(1)}, s32[128]{0:T(128)}, u32[]{:S(2)}) copy-start(s32[128]{0:T(128)} %param.22) | copy-start | bytes 1540
  110.6 53.1 %copy-start.2 = (f32[128]{0:T(128)S(1)}, f32[128]{0:T(128)}, u32[]{:S(2)}) copy-start(f32[128]{0:T(128)} %param.23) | copy-start | bytes 1540
Sparse Core Ops, SparseCore 0:
  48.4 114.5 reduce-scatter.1

commit v7 on v6

--- a/solution.py
+++ b/solution.py
@@ -479,28 +479,6 @@
     columns_stat[...] = jnp.transpose(
         jnp.where(sublane == 0, student_norm, jnp.where(sublane == 1, expect, 0.0))
     )
-    for index, part in enumerate((top, low)):
-        norm = columns_stat[part, :][:, 0:1]
-        mean = columns_stat[part, :][:, 1:2]
-        scale = weight_ref[part, :][:, :1]
-        target, local_max, _, _ = student_side[index]
-        factor = jnp.exp(local_max - norm)
-
-        def gradient(at, first, carry):
-            prob = expo[part, at] * factor
-            picked = (lane + first == target).astype(jnp.float32)
-            grads[part, at] = (
-                scale * (prob * (student[part, at] - logits[part, at] - mean) + picked - prob)
-            ).astype(jnp.bfloat16)
-            return carry
-
-        sweep(gradient, 0)
-
-    for copy in square_copies:
-        copy.wait_send()
-    for copy in head_ring:
-        copy.wait_send()
-
     plan = (
         (grads.at[top], blocks.at[0, top], right),
         (grads.at[low], blocks.at[0, low], right),
@@ -520,8 +498,29 @@
         )
         for i, (source, target, device) in enumerate(plan)
     ]
-    for i in (0, 2, 1, 3):
-        ring[i].start()
+    for index, part in enumerate((top, low)):
+        norm = columns_stat[part, :][:, 0:1]
+        mean = columns_stat[part, :][:, 1:2]
+        scale = weight_ref[part, :][:, :1]
+        target, local_max, _, _ = student_side[index]
+        factor = jnp.exp(local_max - norm)
+
+        def gradient(at, first, carry):
+            prob = expo[part, at] * factor
+            picked = (lane + first == target).astype(jnp.float32)
+            grads[part, at] = (
+                scale * (prob * (student[part, at] - logits[part, at] - mean) + picked - prob)
+            ).astype(jnp.bfloat16)
+            return carry
+
+        sweep(gradient, 0)
+        for i in ((0, 3), (1, 2))[index]:
+            ring[i].start()
+
+    for copy in square_copies:
+        copy.wait_send()
+    for copy in head_ring:
+        copy.wait_send()
 
     def term_copy(slot, side, h, piece):
         return pltpu.make_async_remote_copy(
@@ -673,27 +672,24 @@
     part_width = model_width // tok_count
     student_pair = lax.ppermute(student_head, "tok", [(i, i ^ 1) for i in range(tok_count)])
     teacher_pair = lax.ppermute(teacher_head, "tok", [(i, i ^ 1) for i in range(tok_count)])
-    ids_shares = jnp.concatenate(
-        [expert_ids.astype(jnp.float32), gate_raw, jnp.zeros((rows_here, 128 - 2 * top_k), jnp.float32)],
-        axis=1,
-    )
     rows_all = tok_count * rows_here
-    student_all, tokens_all, table = exchange(
-        [student_hidden, tokens_in, ids_shares],
+    student_all, tokens_all, ids_all, gates_all = exchange(
+        [student_hidden, tokens_in, expert_ids, gate_raw],
         [
             (voc_count,) + student_hidden.shape,
             (tok_count, rows_here, model_width),
-            (tok_count, rows_here, 128),
+            (tok_count, rows_here, top_k),
+            (tok_count, rows_here, top_k),
         ],
-        ("voc", "tok", "tok"),
+        ("voc", "tok", "tok", "tok"),
         2,
-        targets=(at_peer, at_core_chip, at_core_chip),
+        targets=(at_peer, at_core_chip, at_core_chip, at_core_chip),
     )
     student_part = jnp.dot(
         student_all.reshape(-1, part_width), student_head, preferred_element_type=jnp.float32
     )
     tokens_all = tokens_all.reshape(rows_all, model_width)
-    table = table.reshape(rows_all, 128)
+    ids_all = ids_all.reshape(rows_all, top_k)
     slots = 2
     here = voc_count // 2
     column = jnp.arange(here * tok_count * slots, dtype=jnp.int32)
@@ -701,10 +697,10 @@
     column_block = column // slots % tok_count
     column_slot = column % slots
     row = jnp.arange(rows_all, dtype=jnp.int32)
-    gates = table[:, top_k : 2 * top_k]
+    gates = gates_all.reshape(rows_all, top_k)
     shares = gates / jnp.sum(gates, axis=1, keepdims=True)
     named = [
-        table[:, k : k + 1] == column_expert.astype(jnp.float32)[None, :] for k in range(top_k)
+        ids_all[:, k : k + 1] == column_expert[None, :] for k in range(top_k)
     ]
     present = functools.reduce(jnp.logical_or, named)
     share_of = sum(jnp.where(named[k], shares[:, k : k + 1], 0.0) for k in range(top_k))
@@ -734,6 +730,14 @@
         returned.astype(jnp.float32).reshape(here, 2, group, model_width), axis=1
     ).reshape(here * group, model_width)
     mix_part = jnp.dot(combine_table, pair_sum, precision=lax.Precision.HIGHEST)
+    token_count = sampled_ids.shape[0]
+    mix_part, ids_wide, weight_wide = lax.optimization_barrier(
+        (
+            mix_part,
+            jnp.broadcast_to(sampled_ids[:, None], (token_count, 128)),
+            jnp.broadcast_to(token_weight[:, None], (token_count, 128)),
+        )
+    )
     core_rows, chip_width = rows_all // 2, 2 * part_width
     (mix_parts,) = exchange(
         [mix_part.astype(jnp.bfloat16)],
@@ -765,12 +769,11 @@
         8,
         targets=(at_second, at_second),
     )
-    token_count = sampled_ids.shape[0]
     token_loss, hidden_grad = loss_and_grad(
         teacher_rows.reshape(chips, token_count, chip_width),
         squares_rows.reshape(chips, token_count, 128),
-        jnp.broadcast_to(sampled_ids[:, None], (token_count, 128)),
-        jnp.broadcast_to(token_weight[:, None], (token_count, 128)),
+        ids_wide,
+        weight_wide,
         teacher_head,
         teacher_pair,
         student_head,

time: 305 us -> 300 us (0.984)
  transfers between devices with their start and end apart: 3 -> 3, of which waited for: 1 -> 1; matrix products, arithmetic and copies ran while one was open for 3% -> 4% of each run, Pallas kernels for 33% -> 34%
where the time goes in v7:
time: 300 us; the launch traced here: 299 us
  Pallas kernels  253 us (84%)
  matrix products  17 us (6%)
  between operations  14.2 us (5%)
  local copies, waits for them, and re-layouts  7.54 us (3%)
  other arithmetic  5.38 us (2%)
    pallas_call x1, Pallas kernels, loss_and_grad(): pl.pallas_call(loss_kernel, out_shape=(jax.ShapeDtypeStruct((1, count), f...  129 us
    pallas_call x3, Pallas kernels, exchange(): pl.pallas_call(functools.partial(exchange_kernel, axes, sizes, source, ta...  66.3 us
    pallas_call x1, Pallas kernels, expert_layer(): pl.pallas_call(expert_kernel, out_shape=jax.ShapeDtypeStruct((16, group,...  57.7 us
    dot_general x1, matrix products, per_device(): jnp.dot(student_all.reshape(-1, part_width), student_head, preferred_elem...  12.1 us
  transfers between devices with their start and end apart: 3, of which 1 were waited for; matrix products, arithmetic and copies ran while one was open for 4% of the time, Pallas kernels for 34%

profile of v7, /device:TPU:17, one launch (start us, length us, event | category | flops | bytes accessed | tf_op | source)
XLA Modules:
  0.0 299.4 jit_solution(13236412752577311156)
XLA Ops:
  7.2 22.5 %shard_map.131 = (bf16[16,64,512]{2,1,0:T(8,128)(2,1)}, bf16[8,8,4096]{2,1,0:T(8,128)(2,1)}, s32[8,8,8]{2,1,0:T(8,128)}, f32[8,8,8]{2,1,0:T(8,128)}) custom-call(bf16[64,512]{1,0:T(8,128)(2,1)} %refs_0_.1, bf16[8,4096]{1,0:T(8,128)(2,1)} %refs_1_.1, s32[8,8]{1,0:T(8,128)} %refs_2_.1, f32[8,8]{1,0:T(8,128)} %refs_3_.1), custom_call_target="tpu_custom_call" | custom-call | tf_op jit(solution)/shard_map/pallas_call | solution.py:92
  29.7 1.4 fusion.50
  31.1 0.1 copy.23
  31.1 0.1 copy.24
  31.2 0.1 copy.25
  31.3 0.1 copy.26
  31.3 0.1 copy.27
  31.4 0.1 copy.28
  31.6 0.1 copy.30
  31.7 0.3 fusion.1
  32.0 2.5 convolution_convert_fusion
  34.5 12.1 %fusion.51 = f32[1024,4864]{1,0:T(8,128)} fusion(bf16[1024,512]{1,0:T(8,128)(2,1)} %bitcast.67, bf16[512,4864]{1,0:T(8,128)(2,1)} %own_hbm.1), kind=kOutput, calls=%fused_computation.95 | convolution fusion | flops 5100273664 | bytes 25952256 | tf_op jit(solution)/shard_map/dot_general | solution.py:688
  46.6 1.6 collective-permute-start
  48.2 0.3 collective-permute-start.1
  48.5 0.1 reduce_sum.36
  48.6 0.1 div.54
  48.7 57.7 %shard_map.132 = bf16[16,16,4096]{2,1,0:T(8,128)(2,1)} custom-call(bf16[8,16,4096]{2,1,0:T(8,128)(2,1)} %bitcast.45, bf16[4096,384]{1,0:T(8,128)(2,1)} %gate_hbm.1, bf16[4096,384]{1,0:T(8,128)(2,1)} %up_hbm.1, bf16[384,4096]{1,0:T(8,128)(2,1)} %down_hbm.1), custom_call_target="tpu_custom_call" | custom-call | tf_op jit(solution)/shard_map/pallas_call | solution.py:203
  106.4 2.5 convert_reduce_fusion
  109.0 2.1 fusion.11.refs_0_
  111.1 0.7 broadcast_in_dim.126.ids_ref
  111.8 0.7 broadcast_in_dim.127.weight_ref
  112.5 16.8 %shard_map.133 = bf16[8,32,1024]{2,1,0:T(8,128)(2,1)} custom-call(bf16[64,4096]{1,0:T(8,128)(2,1)} %fusion.11.refs_0_), custom_call_target="tpu_custom_call" | custom-call | tf_op jit(solution)/shard_map/pallas_call | solution.py:92
  129.3 0.7 dynamic_slice.7
  130.0 1.1 convert_reduce_fusion.1
  131.2 1.6 multiply_reduce_fusion
  132.8 0.1 broadcast_in_dim.128
  132.9 0.7 broadcast_in_dim.129.refs_1_
  133.6 27.1 %shard_map.134 = (bf16[4,16,8,1024]{3,2,1,0:T(8,128)(2,1)}, f32[4,16,8,128]{3,2,1,0:T(8,128)}) custom-call(bf16[4,8,1024]{2,1,0:T(8,128)(2,1)} %get-tuple-element.29.refs_0_, f32[4,8,128]{2,1,0:T(8,128)} %broadcast_in_dim.129.refs_1_), custom_call_target="tpu_custom_call" | custom-call | tf_op jit(solution)/shard_map/pallas_call | solution.py:92
  160.7 0.6 reduce-scatter.2.cloned.1.call-done.student_hbm
  161.3 128.6 %shard_map.135 = (f32[1,128]{1,0:T(1,128)}, bf16[64,512]{1,0:T(8,128)(2,1)}) custom-call(bf16[4,128,1024]{2,1,0:T(8,128)(2,1)} %bitcast.47, f32[4,128,128]{2,1,0:T(8,128)} %bitcast.49, s32[128,128]{1,0:T(8,128)} %broadcast_in_dim.126.ids_ref, f32[128,128]{1,0:T(8,128)} %broadcast_in_dim.127.weight_ref, bf16[512,4864]{1,0:T(8,128)(2,1)} %head_own_hbm.1, ...), custom_call_target="tpu_custom_call" | custom-call | tf_op jit(solution)/shard_map/pallas_call | solution.py:607
  289.9 1.1 copy.36
  291.0 1.5 copy.37
  (17 shorter events, 0.2 us)
Async XLA Ops:
  7.2 154.2 %reduce-scatter.2.cloned.1.call-start = ((), (), s32[]{:S(2)}) async-start(), calls=%async_computation.1 | async-start | bytes 22413312 | tf_op jit(solution)/shard_map/reduce_scatter | solution.py:725
  46.6 1.9 copy-start
  46.6 114.1 %collective-permute-start = (bf16[512,4864]{1,0:T(8,128)(2,1)}, bf16[512,4864]{1,0:T(8,128)(2,1)}, u32[]{:S(2)}, u32[]{:S(2)}) collective-permute-start(bf16[512,4864]{1,0:T(8,128)(2,1)} %head_own_hbm.1), channel_id=1, source_target_pairs={{0,16},{16,0},{32,48},{48,32},{64,80},{80,64},{96,112},{112,96},{1... | collective-permute-start | bytes 14942216 | tf_op jit(solution)/shard_map/ppermute | solution.py:674
  48.2 112.5 %collective-permute-start.1 = (bf16[512,4864]{1,0:T(8,128)(2,1)}, bf16[512,4864]{1,0:T(8,128)(2,1)}, u32[]{:S(2)}, u32[]{:S(2)}) collective-permute-start(bf16[512,4864]{1,0:T(8,128)(2,1)} %own_hbm.1), channel_id=1, source_target_pairs={{0,16},{16,0},{32,48},{48,32},{64,80},{80,64},{96,112},{112,96},{1... | collective-permute-start | bytes 14942216 | tf_op jit(solution)/shard_map/ppermute | solution.py:673
  106.4 4.7 %copy-start.1 = (s32[128]{0:T(128)S(1)}, s32[128]{0:T(128)}, u32[]{:S(2)}) copy-start(s32[128]{0:T(128)} %param.22) | copy-start | bytes 1540
  106.4 5.4 %copy-start.2 = (f32[128]{0:T(128)S(1)}, f32[128]{0:T(128)}, u32[]{:S(2)}) copy-start(f32[128]{0:T(128)} %param.23) | copy-start | bytes 1540
Sparse Core Ops, SparseCore 0:
  46.7 114.5 reduce-scatter.1
